TPU v7x, 32 devices: a whole 2x2x4 slice. The times are simulated.
32 devices in a mesh: dp: 2 (over y), ctx: 4 (over x, core), tp: 4 (over z).
Axes of the slice: x: 2, y: 2, z: 4, core: 2. Of those that a mesh axis runs over, the one named last changes fastest.
Arguments:
- layer_input: bfloat16 [2, 2048, 1024], P('dp', 'ctx'), may hold values from -6 to 6
- cotangent: bfloat16 [2, 2048, 1024], P('dp', 'ctx'), may hold values from -6 to 6
- segment_ids: int32 [2, 2048], P('dp'), may hold values from 0 to 11, never falling along the last dimension, each value on 1 to 1536 neighbouring positions
- norm1_gain: bfloat16 [1024], P(('dp', 'ctx')), may hold values from 0.5 to 1.5
- norm1_bias: bfloat16 [1024], P(('dp', 'ctx')), may hold values from -3 to 3
- attend_weight: bfloat16 [1024, 3, 1024], P(('dp', 'ctx'), None, 'tp'), may hold values from -0.1875 to 0.1875
- attend_bias: bfloat16 [2, 1024], P(None, ('tp', 'dp', 'ctx')), may hold values from -3 to 3
- merge_weight: bfloat16 [1024, 1024], P('tp', ('dp', 'ctx')), may hold values from -0.75 to 0.75
- merge_bias: bfloat16 [1024], P(('dp', 'ctx')), may hold values from -3 to 3
- norm2_gain: bfloat16 [1024], P(('dp', 'ctx')), may hold values from 0.5 to 1.5
- norm2_bias: bfloat16 [1024], P(('dp', 'ctx')), may hold values from -3 to 3
- expand_weight: bfloat16 [1024, 4096], P(('dp', 'ctx'), 'tp'), may hold values from -0.1875 to 0.1875
- expand_bias: bfloat16 [4096], P(('tp', 'dp', 'ctx')), may hold values from -3 to 3
- shrink_weight: bfloat16 [4096, 1024], P('tp', ('dp', 'ctx')), may hold values from -0.09375 to 0.09375
- shrink_bias: bfloat16 [1024], P(('dp', 'ctx')), may hold values from -3 to 3
Outputs:
- layer_output: bfloat16 [2, 2048, 1024], P('dp', 'ctx')
- input_grad: bfloat16 [2, 2048, 1024], P('dp', 'ctx')
- grad_norm1_gain: float32 [1024], P(('dp', 'ctx'))
- grad_norm1_bias: float32 [1024], P(('dp', 'ctx'))
- grad_attend_weight: float32 [1024, 3, 1024], P(('dp', 'ctx'), None, 'tp')
- grad_attend_bias: float32 [2, 1024], P(None, ('tp', 'dp', 'ctx'))
- grad_merge_weight: float32 [1024, 1024], P('tp', ('dp', 'ctx'))
- grad_merge_bias: float32 [1024], P(('dp', 'ctx'))
- grad_norm2_gain: float32 [1024], P(('dp', 'ctx'))
- grad_norm2_bias: float32 [1024], P(('dp', 'ctx'))
- grad_expand_weight: float32 [1024, 4096], P(('dp', 'ctx'), 'tp')
- grad_expand_bias: float32 [4096], P(('tp', 'dp', 'ctx'))
- grad_shrink_weight: float32 [4096, 1024], P('tp', ('dp', 'ctx'))
- grad_shrink_bias: float32 [1024], P(('dp', 'ctx'))
Inputs may be any that keep to these rules, and one draw needn't show every extreme that they name: `segment_ids`: within each sequence the segment number never falls; every number 0 to 11 occurs; each holds 1 to 1536 tokens and one holds exactly 1536; segment 0, at the start of a sequence, is padding.
All inputs are finite; a program needn't handle non-finite values.
Results may differ from a plain program's by a relative error of at most 0.02.
Values may be sent and summed in bfloat16 or wider, within the bound.
No kernel may reach another device: no remote copies, remote signals or barrier semaphores. Data moves between devices by JAX's collectives and lax.ppermute only.
A program may use at most 128 MiB of HBM per device.

v0:
```python
import functools

import jax
import jax.numpy as jnp
from jax import lax
from jax.experimental import pallas as pl
from jax.experimental.pallas import tpu as pltpu
from jax.sharding import PartitionSpec as P

HD = 64
NEG = -1e30
F32 = jnp.float32
BF16 = jnp.bfloat16


def dot(left, right, left_dim, right_dim):
    return lax.dot_general(
        left, right, (((left_dim,), (right_dim,)), ((), ())), preferred_element_type=F32
    )


def shape(dims, dtype):
    return jax.ShapeDtypeStruct(tuple(dims), dtype)


def call(kernel, name, scalars, ins, outs, scratch=(), flops=0, whole=None):
    first = [] if scalars is None else [scalars]
    specs, arrays, moved = [], [], 0
    for value in ins:
        if isinstance(value, tuple):
            value, dims, index = value
            specs.append(pl.BlockSpec(dims, lambda i, index=index: index))
            moved += value.dtype.itemsize * functools.reduce(lambda a, b: a * b, dims)
        else:
            specs.append(pl.BlockSpec(memory_space=pltpu.VMEM))
            moved += value.size * value.dtype.itemsize
        arrays.append(value)
    moved += sum(v.size * v.dtype.itemsize for v in outs)
    out_specs = [pl.BlockSpec(memory_space=pltpu.VMEM)] * len(outs)
    alias = {}
    if whole is not None:
        alias = {len(first) + len(arrays): len(outs)}
        specs.append(pl.BlockSpec(memory_space=pl.ANY))
        arrays.append(whole)
        outs = [*outs, shape(whole.shape, whole.dtype)]
        out_specs.append(pl.BlockSpec(memory_space=pl.ANY))
    return pl.pallas_call(
        kernel,
        grid=(1,),
        out_shape=tuple(outs),
        in_specs=[pl.BlockSpec(memory_space=pltpu.SMEM)] * len(first) + specs,
        out_specs=tuple(out_specs),
        input_output_aliases=alias,
        scratch_shapes=list(scratch),
        compiler_params=pltpu.CompilerParams(vmem_limit_bytes=56 << 20),
        cost_estimate=pl.CostEstimate(
            flops=flops, transcendentals=0, bytes_accessed=moved
        ),
        name=name,
    )(*first, *arrays)


def lanes(index, offset, size):
    return pl.ds(pl.multiple_of((index ^ offset) * size, size), size)


def rows_of(refs, low, high):
    return jnp.concatenate([ref[low:high, :] for ref in refs], axis=0)


def pack_kernel(attend_ref, *refs):
    smalls, (pair_ref, out_ref) = refs[:-2], refs[-2:]
    parts, block, width = attend_ref.shape
    for c in range(parts):
        out_ref[:block, c * width : (c + 1) * width] = attend_ref[c]
    size = smalls[0].shape[1]
    last = jnp.concatenate([pair_ref[0:1, :], pair_ref[1:2, :]], axis=1).astype(F32)
    last = jnp.concatenate([last, jnp.zeros((1, size - last.shape[1]), F32)], axis=1)
    rows = jnp.concatenate([ref[...].astype(F32) for ref in smalls] + [last], axis=0)
    out_ref[block:, :size] = rows.astype(BF16)
    out_ref[block:, size:] = jnp.zeros((8, parts * width - size), BF16)


def turn_kernel(expand_ref, shrink_ref, out_ref):
    block = expand_ref.shape[0]
    out_ref[:block, :] = expand_ref[...]
    out_ref[block:, :] = shrink_ref[...].T


def decode(order, head_block, index, first, start, size, wide_ref, expand_ref, attend_ref):
    total = jnp.zeros(attend_ref.shape, F32)
    for place, offset in enumerate(order):
        rows = first[place][start : start + 8, :size].astype(F32)
        wide_ref[:, place * size : (place + 1) * size] = rows
        expand_ref[:, lanes(index, offset, size)] = rows[6:7, :]
        flat = jnp.concatenate([rows[7:8, :head_block], rows[7:8, head_block : 2 * head_block]], 0)
        flat = jnp.concatenate(
            [flat, jnp.zeros((2, attend_ref.shape[1] - head_block), F32)], axis=1
        )
        flat = jnp.concatenate([flat, jnp.zeros((6, attend_ref.shape[1]), F32)], axis=0)
        total = total + pltpu.roll(flat, (index ^ offset) * head_block, 1)[:2]
    attend_ref[...] = total


def grad_order_kernel(order, count, scalars, cot_ref, keep_ref, *outs):
    index, tp = scalars[0], scalars[2]
    height, wide = outs[0].shape
    size = wide // len(order)
    for o in range(count):
        rows = pl.ds(pl.multiple_of((tp ^ o) * height, height), height)
        keep = keep_ref[rows, 0:1]
        for place, offset in enumerate(order):
            outs[o][:, place * size : (place + 1) * size] = (
                cot_ref[rows, lanes(index, offset, size)] * keep
            )


def project_kernel(order, block, head_block, scalars, x_ref, *refs):
    count = len(order)
    weights, refs = refs[:count], refs[count:]
    given, outs = refs[:-7], refs[-7:]
    normed_ref, query_ref, pair_ref, rows_ref = outs[:4]
    wide_ref, expand_ref, attend_ref = outs[4:]
    index, tp = scalars[0], scalars[2]
    q_len, wide = x_ref.shape
    size = wide // count
    for source, target in zip(given, outs[4:]):
        target[...] = source[...]
    if not given:
        decode(order, head_block, index, weights, block, size, wide_ref, expand_ref, attend_ref)
    width = query_ref.shape[1]
    weight = rows_of(weights, 0, block)
    step = min(q_len, 256)
    bias = jnp.concatenate(
        [attend_ref[0:1, :], jnp.zeros((1, width), F32), attend_ref[1:2, :]], axis=1
    )
    for start in range(0, q_len, step):
        rows = slice(start, start + step)
        value = x_ref[rows, :].astype(F32)
        mean = jnp.mean(value, axis=-1, keepdims=True)
        centered = value - mean
        inv = lax.rsqrt(jnp.mean(centered * centered, axis=-1, keepdims=True) + 1e-05)
        for place, offset in enumerate(order):
            plain = slice(place * size, (place + 1) * size)
            part = x_ref[rows, lanes(index, offset, size)].astype(F32)
            part = (part - mean) * inv * wide_ref[0:1, plain] + wide_ref[1:2, plain]
            normed_ref[rows, plain] = part.astype(BF16)
        made = dot(normed_ref[rows, :], weight, 1, 0) + bias
        query_ref[rows, :] = made[:, :width].astype(BF16)
        pair_ref[rows, :] = made[:, width:].astype(BF16)
    height = rows_ref.shape[0]
    mine = pl.ds(pl.multiple_of(tp * height, height), height)
    for place, offset in enumerate(order):
        plain = slice(place * size, (place + 1) * size)
        rows_ref[:, plain] = x_ref[mine, lanes(index, offset, size)]


def attend_kernel(heads, tq, tk, n_chunk, n_tp, scalars, lo_ref, q_ref, *refs):
    kv_refs = refs[:n_chunk]
    outs, refs = refs[n_chunk : n_chunk + n_tp], refs[n_chunk + n_tp :]
    lse_ref, qm_ref, acc_ref, m_ref, l_ref, mixed_ref = refs
    q_len, width = q_ref.shape
    ctx = scalars[1]
    lane = lax.broadcasted_iota(jnp.int32, (tq, width), 1)

    def tile(qi, carry):
        rows = pl.ds(pl.multiple_of(qi * tq, tq), tq)
        qv = q_ref[rows, :] * BF16(0.125)
        for h in range(heads):
            mine = (lane >= h * HD) & (lane < (h + 1) * HD)
            qm_ref[h * tq : (h + 1) * tq, :] = jnp.where(mine, qv, jnp.zeros_like(qv))
        acc_ref[...] = jnp.zeros_like(acc_ref)
        m_ref[...] = jnp.full(m_ref.shape, NEG, F32)
        l_ref[...] = jnp.zeros_like(l_ref)
        qbase = ctx * q_len + qi * tq
        qpos = qbase + lax.broadcasted_iota(jnp.int32, (1, tq), 1)
        lo = lo_ref[0:1, rows]
        lo_first = scalars[3 + qi]
        for c in range(n_chunk):
            kv = kv_refs[c]
            cbase = (ctx ^ c) * q_len

            def step(ki, carry, kv=kv, cbase=cbase):
                kb = cbase + ki * tk

                @pl.when((kb <= qbase + tq - 1) & (kb + tk - 1 >= lo_first))
                def _():
                    krows = pl.ds(pl.multiple_of(ki * tk, tk), tk)
                    k = kv[krows, 0:width]
                    vt = kv[krows, width : 2 * width].T
                    kpos = kb + lax.broadcasted_iota(jnp.int32, (tk, 1), 0)
                    ok = (kpos >= lo) & (kpos <= qpos)
                    ok = jnp.concatenate([ok] * heads, axis=1)
                    s = jnp.where(ok, dot(k, qm_ref[...], 1, 1), NEG)
                    m0 = m_ref[...]
                    m1 = jnp.maximum(m0, jnp.max(s, axis=0, keepdims=True))
                    p = jnp.exp(s - m1)
                    al = jnp.exp(m0 - m1)
                    l_ref[...] = l_ref[...] * al + jnp.sum(p, axis=0, keepdims=True)
                    m_ref[...] = m1
                    low = p.astype(BF16)
                    made = [
                        dot(vt[h * HD : (h + 1) * HD, :], low[:, h * tq : (h + 1) * tq], 1, 0)
                        for h in range(heads)
                    ]
                    acc_ref[...] = acc_ref[...] * al + jnp.concatenate(made, axis=1)

                return carry

            lax.fori_loop(0, q_len // tk, step, 0)
        lse = m_ref[...] + jnp.log(l_ref[...])
        out = acc_ref[...] / l_ref[...]
        for h in range(heads):
            cols = slice(h * tq, (h + 1) * tq)
            lse_ref[h : h + 1, rows] = lse[:, cols]
        out = jnp.concatenate([out[:, h * tq : (h + 1) * tq] for h in range(heads)], axis=0)
        mixed_ref[rows, :] = out.T.astype(BF16)
        return carry

    lax.fori_loop(0, q_len // tq, tile, 0)
    for o in range(n_tp):
        outs[o][...] = mixed_ref[lanes(scalars[2], o, q_len // n_tp), :]


def attend_back_kernel(heads, tq, tk, n_chunk, n_tp, scalars, lo_ref, lse_ref, q_ref, *refs):
    kv_refs, refs = refs[:n_chunk], refs[n_chunk:]
    mixed_refs, refs = refs[:n_tp], refs[n_tp:]
    gm_refs, refs = refs[:n_tp], refs[n_tp:]
    dq_ref, refs = refs[0], refs[1:]
    dkv_refs, refs = refs[:n_chunk], refs[n_chunk:]
    qm_ref, gom_ref, dqt_ref, acck_ref, accv_ref, go_ref, mixed_ref, row_ref = refs
    q_len, width = q_ref.shape
    ctx, tp = scalars[1], scalars[2]
    for o in range(n_tp):
        go_ref[lanes(tp, o, q_len // n_tp), :] = gm_refs[o][...]
        mixed_ref[lanes(tp, o, q_len // n_tp), :] = mixed_refs[o][...]
    lane = lax.broadcasted_iota(jnp.int32, (tq, width), 1)
    nq = q_len // tq

    def ready(qi, carry):
        rows = pl.ds(pl.multiple_of(qi * tq, tq), tq)
        qv = q_ref[rows, :] * BF16(0.125)
        gv = go_ref[rows, :]
        prod = (gv.astype(F32) * mixed_ref[rows, :].astype(F32)).T
        for h in range(heads):
            cols = slice(h * tq, (h + 1) * tq)
            mine = (lane >= h * HD) & (lane < (h + 1) * HD)
            qm_ref[qi, cols, :] = jnp.where(mine, qv, jnp.zeros_like(qv))
            gom_ref[qi, cols, :] = jnp.where(mine, gv, jnp.zeros_like(gv))
            row_ref[qi, 0:1, cols] = lse_ref[h : h + 1, rows]
            row_ref[qi, 1:2, cols] = jnp.sum(
                prod[h * HD : (h + 1) * HD, :], axis=0, keepdims=True
            )
        return carry

    lax.fori_loop(0, nq, ready, 0)
    dqt_ref[...] = jnp.zeros_like(dqt_ref)
    for c in range(n_chunk):
        kv = kv_refs[c]
        dkv = dkv_refs[c]
        cbase = (ctx ^ c) * q_len

        def step(ki, carry, kv=kv, dkv=dkv, cbase=cbase):
            kb = cbase + ki * tk
            krows = pl.ds(pl.multiple_of(ki * tk, tk), tk)
            live = [
                (kb <= ctx * q_len + (qi + 1) * tq - 1) & (kb + tk - 1 >= scalars[3 + qi])
                for qi in range(nq)
            ]
            some = functools.reduce(jnp.logical_or, live)

            @pl.when(jnp.logical_not(some))
            def _():
                dkv[krows, :] = jnp.zeros((tk, 2 * width), BF16)

            @pl.when(some)
            def _():
                acck_ref[...] = jnp.zeros_like(acck_ref)
                accv_ref[...] = jnp.zeros_like(accv_ref)
                k = kv[krows, 0:width]
                v = kv[krows, width : 2 * width]
                kt = k.T
                kpos = kb + lax.broadcasted_iota(jnp.int32, (tk, 1), 0)

                def tile(qi, carry):
                    qbase = ctx * q_len + qi * tq

                    @pl.when((kb <= qbase + tq - 1) & (kb + tk - 1 >= scalars[3 + qi]))
                    def _():
                        rows = pl.ds(pl.multiple_of(qi * tq, tq), tq)
                        qpos = qbase + lax.broadcasted_iota(jnp.int32, (1, tq), 1)
                        ok = (kpos >= lo_ref[0:1, rows]) & (kpos <= qpos)
                        ok = jnp.concatenate([ok] * heads, axis=1)
                        s = dot(k, qm_ref[qi], 1, 1)
                        dp = dot(v, gom_ref[qi], 1, 1)
                        p = jnp.where(ok, jnp.exp(s - row_ref[qi, 0:1, :]), 0.0)
                        ds = (p * (dp - row_ref[qi, 1:2, :])).astype(BF16)
                        accv_ref[...] += dot(p.astype(BF16), gom_ref[qi], 1, 0)
                        acck_ref[...] += dot(ds, qm_ref[qi], 1, 0)
                        for h in range(heads):
                            hs = slice(h * HD, (h + 1) * HD)
                            dqt_ref[hs, rows] += dot(
                                kt[hs, :], ds[:, h * tq : (h + 1) * tq], 1, 0
                            )

                    return carry

                lax.fori_loop(0, nq, tile, 0)
                dkv[krows, 0:width] = acck_ref[...].astype(BF16)
                dkv[krows, width : 2 * width] = accv_ref[...].astype(BF16)

            return carry

        lax.fori_loop(0, q_len // tk, step, 0)
    for qi in range(nq):
        rows = slice(qi * tq, (qi + 1) * tq)
        dq_ref[rows, :] = (dqt_ref[:, rows].T * 0.125).astype(BF16)


def attend_scratch(heads, tile, q_len, width):
    return [
        pltpu.VMEM((heads * tile, width), BF16),
        pltpu.VMEM((HD, heads * tile), F32),
        pltpu.VMEM((1, heads * tile), F32),
        pltpu.VMEM((1, heads * tile), F32),
        pltpu.VMEM((q_len, width), BF16),
    ]


def attend_back_scratch(heads, tile, span, q_len, width):
    return [
        pltpu.VMEM((q_len // tile, heads * tile, width), BF16),
        pltpu.VMEM((q_len // tile, heads * tile, width), BF16),
        pltpu.VMEM((width, q_len), F32),
        pltpu.VMEM((span, width), F32),
        pltpu.VMEM((span, width), F32),
        pltpu.VMEM((q_len, width), BF16),
        pltpu.VMEM((q_len, width), BF16),
        pltpu.VMEM((q_len // tile, 2, heads * tile), F32),
    ]


def normal(value):
    mean = jnp.mean(value, axis=-1, keepdims=True)
    centered = value - mean
    inv = lax.rsqrt(jnp.mean(centered * centered, axis=-1, keepdims=True) + 1e-05)
    return centered * inv, inv


def normal_back(grad_out, norm, inv, gain):
    grad = grad_out * gain
    centered = grad - jnp.mean(grad, axis=-1, keepdims=True)
    return inv * (centered - norm * jnp.mean(grad * norm, axis=-1, keepdims=True))


def merge_kernel(n_tp, order, scalars, rows_ref, wide_ref, weight_ref, *refs):
    mixed, (hidden_ref, normed_ref) = refs[:n_tp], refs[n_tp:]
    index, tp = scalars[0], scalars[2]
    hidden_ref[...] = rows_ref[...].astype(F32) + wide_ref[2:3, :]
    for o, ref in enumerate(mixed):
        weight = jnp.concatenate([weight_ref[index ^ p, tp ^ o] for p in order], axis=1)
        hidden_ref[...] += dot(ref[...], weight, 1, 0)
    norm, _ = normal(hidden_ref[...])
    normed_ref[...] = (norm * wide_ref[3:4, :] + wide_ref[4:5, :]).astype(BF16)


def dense_kernel(count, expand_ref, *refs):
    normed, refs = refs[:count], refs[count:]
    grads, refs = refs[:count], refs[count:]
    weights, outs = refs[: -4 * count - 1], refs[-4 * count - 1 :]
    acts, pres, normed_outs, mlp_outs = (outs[i * count : (i + 1) * count] for i in range(4))
    sum_ref = outs[-1]
    block = weights[0].shape[0] // 2
    height = normed[0].shape[0]
    hidden = expand_ref.shape[1]
    step = min(hidden, 512)
    value = jnp.concatenate([ref[...] for ref in normed], axis=0)
    grad = jnp.concatenate([ref[...] for ref in grads], axis=0)
    back = forth = None
    for start in range(0, hidden, step):
        cols = slice(start, start + step)
        expand = jnp.concatenate([ref[:block, cols] for ref in weights], axis=0)
        shrink = jnp.concatenate([ref[block:, cols] for ref in weights], axis=0)
        pre = dot(value, expand, 1, 0) + expand_ref[:, cols]
        square = pre * pre
        inner = jnp.tanh(0.7978845608028654 * (pre + 0.044715 * square * pre))
        act = (0.5 * pre * (1.0 + inner)).astype(BF16)
        slope = 0.5 * (1.0 + inner) + (0.5 * 0.7978845608028654) * pre * (
            1.0 - inner * inner
        ) * (1.0 + (3.0 * 0.044715) * square)
        low = (dot(grad, shrink, 1, 0) * slope).astype(BF16)
        sum_ref[:, cols] = jnp.sum(low.astype(F32), axis=0, keepdims=True)
        for i in range(count):
            rows = slice(i * height, (i + 1) * height)
            acts[i][:, cols] = act[rows]
            pres[i][:, cols] = low[rows]
        more = dot(low, expand, 1, 1)
        also = dot(act, shrink, 1, 1)
        back = more if back is None else back + more
        forth = also if forth is None else forth + also
    for i in range(count):
        rows = slice(i * height, (i + 1) * height)
        normed_outs[i][...] = back[rows].astype(BF16)
        mlp_outs[i][...] = forth[rows].astype(BF16)


def hidden_back_kernel(
    count, n_tp, order, scalars, grad_ref, hidden_ref, wide_ref, weight_ref, *refs
):
    parts, refs = refs[:count], refs[count:]
    mixed, refs = refs[:n_tp], refs[n_tp:]
    direct = len(order) > 1
    refs = refs[1:] if direct else refs
    back_ref, low_ref, sums_ref = refs[:3]
    outs, refs = refs[3 : 3 + n_tp], refs[3 + n_tp :]
    index, tp = scalars[0], scalars[2]
    total = total_of(parts)
    norm, inv = normal(hidden_ref[...])
    grad = grad_ref[...].astype(F32)
    back = grad + normal_back(total, norm, inv, wide_ref[3:4, :])
    back_ref[...] = back
    low = back.astype(BF16)
    low_ref[...] = low
    copies = []
    if direct:
        buffer_ref, made_ref, sems = refs
        values = jnp.concatenate([ref[...] for ref in mixed], axis=1)
        tall = made_ref.shape[1]
        for place, offset in enumerate(order):
            left = low[:, place * tall : (place + 1) * tall]
            made_ref[place] = dot(left, values, 0, 0).astype(BF16)
            copies.append(
                pltpu.make_async_copy(
                    made_ref.at[place],
                    buffer_ref.at[index ^ offset, pl.ds(2 * tall, tall), :],
                    sems.at[place],
                )
            )
            copies[-1].start()
    for o in range(n_tp):
        weight = jnp.concatenate([weight_ref[index ^ p, tp ^ o] for p in order], axis=1)
        outs[o][...] = dot(low, weight, 1, 1).astype(BF16)
    sums_ref[...] = jnp.concatenate(
        [jnp.sum(v, axis=0, keepdims=True) for v in (back, total * norm, total, grad)], axis=0
    )
    for copy in copies:
        copy.wait()


def outer_kernel(order, spans, scalars, *refs):
    out_ref = refs[-1]
    tall = out_ref.shape[1] // (len(spans) + 1)
    base = 0
    for many, more in spans:
        left, refs = refs[:many], refs[many:]
        right, refs = refs[:more], refs[more:]
        a = jnp.concatenate([ref[...] for ref in left], axis=0)
        b = jnp.concatenate([ref[...] for ref in right], axis=0)
        for place, offset in enumerate(order):
            made = dot(a[:, place * tall : (place + 1) * tall], b, 0, 0).astype(BF16)
            out_ref[scalars[0] ^ offset, base : base + tall, :] = made
        base += tall


def join_kernel(left_ref, right_ref, out_ref):
    total = left_ref[...].astype(F32) + right_ref[...].astype(F32)
    out_ref[...] = total.astype(out_ref.dtype)


def sum_of(ref):
    total = ref[0].astype(F32)
    for i in range(1, ref.shape[0]):
        total = total + ref[i].astype(F32)
    return total


def dense_total_kernel(in_ref, expand_ref, shrink_ref, *outs):
    block = expand_ref.shape[0]
    expand_ref[...] = in_ref[:block, :].astype(F32)
    shrink_ref[...] = in_ref[block : 2 * block, :].astype(F32).T
    width = outs[0].shape[1]
    for o, ref in enumerate(outs):
        ref[...] = in_ref[2 * block :, o * width : (o + 1) * width]


def attend_total_kernel(in_ref, out_ref):
    parts, _, width = out_ref.shape
    for c in range(parts):
        out_ref[c] = in_ref[:, c * width : (c + 1) * width].astype(F32)


def total_of(refs):
    total = refs[0][...].astype(F32)
    for ref in refs[1:]:
        total = total + ref[...].astype(F32)
    return total


def join_layer_kernel(order, scalars, left_ref, right_ref, hidden_ref, wide_ref, *refs):
    total = left_ref[...].astype(F32) + right_ref[...].astype(F32)
    refs[-2][...] = total.astype(BF16)
    value = (hidden_ref[...] + total_of(refs[:-2]) + wide_ref[5:6, :]).astype(BF16)
    size = value.shape[1] // len(order)
    for place, offset in enumerate(order):
        cols = slice(place * size, (place + 1) * size)
        refs[-1][:, lanes(scalars[0], offset, size)] = value[:, cols]


def input_kernel(order, count, scalars, rows_ref, back_ref, wide_ref, *refs):
    parts, refs = refs[:count], refs[count:]
    extra, outs = refs[: len(refs) - count], refs[len(refs) - count :]
    total = total_of(parts)
    norm, inv = normal(rows_ref[...].astype(F32))
    value = (back_ref[...] + normal_back(total, norm, inv, wide_ref[0:1, :])).astype(BF16)
    height, wide = value.shape
    size = wide // len(order)
    for o, out_ref in enumerate(outs):
        for place, offset in enumerate(order):
            cols = lanes(scalars[0], offset, size)
            out_ref[:height, cols] = value[:, place * size : (place + 1) * size]
        if extra:
            tall, width = extra[o].shape
            tall = tall * width // wide
            for j in range(wide // width):
                out_ref[height:, j * width : (j + 1) * width] = extra[o][
                    j * tall : (j + 1) * tall, :
                ]


def first_sums_kernel(order, scalars, x_ref, *refs):
    parts, out_ref = refs[:-1], refs[-1]
    height, wide = parts[0].shape
    size = wide // len(order)
    out_ref[...] = jnp.zeros_like(out_ref)
    for o, ref in enumerate(parts):
        rows = lanes(scalars[2], o, height)
        value = x_ref[rows, :].astype(F32)
        mean = jnp.mean(value, axis=-1, keepdims=True)
        centered = value - mean
        inv = lax.rsqrt(jnp.mean(centered * centered, axis=-1, keepdims=True) + 1e-05)
        for place, offset in enumerate(order):
            cols = slice(place * size, (place + 1) * size)
            part = ref[:, cols].astype(F32)
            norm = (x_ref[rows, lanes(scalars[0], offset, size)].astype(F32) - mean) * inv
            out_ref[0:1, cols] += jnp.sum(part * norm, axis=0, keepdims=True)
            out_ref[1:2, cols] += jnp.sum(part, axis=0, keepdims=True)


def place_kernel(count, height, scalars, *refs):
    parts, outs = refs[:count], refs[count:]
    wide = parts[0].shape[1]
    for o, ref in enumerate(parts):
        outs[0][lanes(scalars[2], o, height), :] = ref[:height, :]
    if len(outs) > 1:
        width = outs[1].shape[0]
        tall = parts[0].shape[0] - height
        total = total_of([ref.at[height:, :] for ref in parts])
        for j in range(wide // width):
            outs[1][:, j * tall : (j + 1) * tall] = total[:, j * width : (j + 1) * width].T


def project_back_kernel(block, order, n_pair, n_tp, scalars, normed_ref, dq_ref, *refs):
    joined, refs = refs[:n_pair], refs[n_pair:]
    weights, refs = refs[: len(order)], refs[len(order) :]
    outs, (pair_ref, sums_ref, outer_ref) = refs[:n_tp], refs[n_tp:]
    pair = total_of(joined).astype(BF16)
    pair_ref[...] = pair
    width = dq_ref.shape[1]
    weight = rows_of(weights, 0, block)
    height = outs[0].shape[0]
    for o in range(n_tp):
        rows = lanes(scalars[2], o, height)
        both = jnp.concatenate([dq_ref[rows, :], pair_ref[rows, :]], axis=1)
        outs[o][...] = dot(both, weight, 1, 1).astype(BF16)
    sums_ref[...] = jnp.concatenate(
        [
            jnp.sum(v, axis=0, keepdims=True)
            for v in (dq_ref[...].astype(F32), pair[:, width:].astype(F32))
        ],
        axis=0,
    )
    tall = outer_ref.shape[1]
    both = jnp.concatenate([dq_ref[...], pair], axis=1)
    for place, offset in enumerate(order):
        rows = slice(place * tall, (place + 1) * tall)
        outer_ref[scalars[0] ^ offset] = dot(normed_ref[:, rows], both, 0, 0).astype(BF16)


def add_kernel(left_ref, right_ref, out_ref):
    out_ref[...] = left_ref[...].astype(F32) + right_ref[...].astype(F32)


def small_kernel(order, head_block, n_tp, scalars, two_ref, four_ref, attend_ref, *refs):
    index = scalars[0]
    out_ref = refs[-1]
    hidden = total_of(refs[:-1])
    size = out_ref.shape[2]
    attend = jnp.concatenate([attend_ref[...], jnp.zeros((6, attend_ref.shape[1]), F32)], axis=0)
    for place, offset in enumerate(order):
        cols = slice(place * size, (place + 1) * size)
        block = index ^ offset
        turned = pltpu.roll(attend, attend.shape[1] - block * head_block, 1)
        last = jnp.concatenate(
            [
                turned[0:1, :head_block],
                turned[1:2, :head_block],
                jnp.zeros((1, size - 2 * head_block), F32),
            ],
            axis=1,
        )
        mine = jnp.zeros((1, size), F32)
        for j in range(len(order)):
            mine = mine + jnp.where(block == j, hidden[:, j * size : (j + 1) * size], 0.0)
        made = jnp.concatenate([two_ref[:, cols], four_ref[:, cols], mine, last], axis=0)
        for o in range(n_tp):
            out_ref[block * n_tp + o] = made


def small_total_kernel(n_tp, scalars, in_ref, *outs):
    total = sum_of(in_ref)
    local = in_ref[scalars[2]]
    for i in range(1, in_ref.shape[0] // n_tp):
        local = local + in_ref[i * n_tp + scalars[2]]
    for i in range(6):
        outs[i][...] = total[i : i + 1, :]
    outs[6][...] = local[6:7, :]
    size = outs[7].shape[1]
    outs[7][...] = jnp.concatenate([local[7:8, :size], local[7:8, size : 2 * size]], axis=0)


def after(value, *others):
    return lax.optimization_barrier((value, *others))[0]


def body(
    sizes,
    layer_input,
    cotangent,
    segment_ids,
    norm1_gain,
    norm1_bias,
    attend_weight,
    attend_bias,
    merge_weight,
    merge_bias,
    norm2_gain,
    norm2_bias,
    expand_weight,
    expand_bias,
    shrink_weight,
    shrink_bias,
):
    n_dp, n_ctx, n_tp = sizes
    group = n_dp * n_ctx
    seqs, q_len, wide = layer_input.shape
    assert seqs == 1
    block = wide // group
    width = attend_weight.shape[2]
    heads = width // HD
    hidden_width = expand_weight.shape[1]
    height = q_len // n_tp
    bias_block = expand_bias.shape[0]
    head_block = attend_bias.shape[1]
    tile = min(256, q_len)
    direct = (n_dp, n_ctx) == (2, 4) and block % 128 == 0
    direct = direct and bias_block == block and 2 * head_block <= block
    order = [0, 2, 4, 6, 1, 3, 5, 7] if direct else [0]
    ctx = lax.axis_index("ctx")
    tp = lax.axis_index("tp")
    me = lax.axis_index("dp") * n_ctx + ctx if direct else 0 * ctx
    plane = ("dp", "ctx")

    def plane_swap(value, offset):
        return lax.ppermute(value, plane, [(i, i ^ offset) for i in range(group)])

    def ctx_swap(value, offset):
        return lax.ppermute(value, "ctx", [(i, i ^ offset) for i in range(n_ctx)])

    def tp_swap(value, offset):
        return lax.ppermute(value, "tp", [(i, i ^ offset) for i in range(n_tp)])

    def with_cores(even):
        return even + [ctx_swap(v, 1) for v in even]

    def tp_gather(value):
        return [value] + [tp_swap(value, o) for o in range(1, n_tp)]

    def tp_relay(value):
        parts = [value, tp_swap(value, 1)]
        for step in (2 ** i for i in range(1, n_tp.bit_length() - 1)):
            far = tp_swap(value, step)
            parts += [far, tp_swap(far, 1)] + [tp_swap(value, o) for o in range(step + 2, 2 * step)]
        return parts

    def tp_exchange(parts):
        return [parts[0]] + [tp_swap(parts[o], o) for o in range(1, n_tp)]

    seg_all = segment_ids[0]
    seg_query = lax.dynamic_slice_in_dim(seg_all, ctx * q_len, q_len, 0)
    lows = jnp.sum(
        (seg_all[:, None] < seg_query[None, :]).astype(jnp.int32), axis=0, keepdims=True
    )
    place = jnp.stack([me, ctx, tp]).astype(jnp.int32)
    limits = jnp.concatenate([place, lows[0, ::tile]], axis=0)
    keep = jnp.broadcast_to((seg_query > 0).astype(BF16)[:, None], (q_len, 128))

    smalls = (
        norm1_gain,
        norm1_bias,
        merge_bias,
        norm2_gain,
        norm2_bias,
        shrink_bias,
        expand_bias,
    )
    if direct:
        (pack,) = call(
            pack_kernel,
            "pack",
            None,
            [jnp.swapaxes(attend_weight, 0, 1)]
            + [jnp.reshape(v, (1, block)) for v in smalls]
            + [attend_bias],
            [shape((block + 8, 3 * width), BF16)],
        )
        far = [plane_swap(pack, o) for o in order[1:4]]
        first = with_cores([after(v, limits, keep) for v in [pack] + far])
        merge_all = lax.all_gather(merge_weight, ("dp", "ctx", "tp"), axis=0)
        merge_all = jnp.reshape(merge_all, (group, n_tp, width, block))
        given = []
    else:

        def whole(value, axis):
            return lax.all_gather(value, plane, axis=axis, tiled=True)

        first = [jnp.reshape(whole(attend_weight, 0), (wide, 3 * width))]
        merge_all = whole(lax.all_gather(merge_weight, "tp", axis=0), 2)[None]
        dense_all = [jnp.concatenate([whole(expand_weight, 0), whole(shrink_weight.T, 0)], 0)]
        wide_rows = whole(jnp.stack(smalls[:6]), 1).astype(F32)
        given = [
            jnp.pad(wide_rows, ((0, 2), (0, 0))),
            whole(expand_bias, 0).astype(F32)[None],
            whole(attend_bias, 1).astype(F32),
        ]
    span = block if direct else wide

    normed1, query, pair, input_rows, wide_rows, expand_add, attend_add = call(
        functools.partial(project_kernel, order, span, head_block),
        "project",
        place,
        [layer_input[0], *first, *given],
        [
            shape((q_len, wide), BF16),
            shape((q_len, width), BF16),
            shape((q_len, 2 * width), BF16),
            shape((height, wide), BF16),
            shape((8, wide), F32),
            shape((1, hidden_width), F32),
            shape((2, width), F32),
        ],
        flops=6 * q_len * wide * width,
    )
    grad_rows = call(
        functools.partial(grad_order_kernel, order, n_tp),
        "order_grad",
        place,
        [after(cotangent[0], pair), keep],
        [shape((height, wide), BF16)] * n_tp,
    )
    ready = [grad_rows[0], limits]
    if direct:
        (dense_rows,) = call(
            turn_kernel,
            "turn",
            None,
            [after(expand_weight, pair), shrink_weight],
            [shape((2 * block, hidden_width), BF16)],
        )
        ready.append(dense_rows)
    near = [pair] + [ctx_swap(pair, o) for o in range(2, n_ctx, 2)]
    pairs = []
    for value in near:
        if pairs:
            value = after(value, *ready)
        pairs += [value, ctx_swap(value, 1)]
    if direct:
        dense_y = plane_swap(dense_rows, 4)
        dense_core = ctx_swap(dense_rows, 1)
        pairs[-1] = after(pairs[-1], dense_y, dense_core)
        dense_x, dense_xy = (plane_swap(after(dense_rows, near[1]), o) for o in (2, 6))
    out = call(
        functools.partial(attend_kernel, heads, tile, min(512, q_len), n_ctx, n_tp),
        "attention",
        limits,
        [lows, query, *pairs],
        [shape((height, width), BF16)] * n_tp + [shape((heads, q_len), F32)],
        attend_scratch(heads, tile, q_len, width),
        flops=4 * q_len * q_len * n_ctx * width,
    )
    mixed, lse = out[:n_tp], out[n_tp]
    mixed_rows = tp_exchange(mixed)
    hidden, normed2 = call(
        functools.partial(merge_kernel, n_tp, order),
        "merge",
        place,
        [input_rows, wide_rows, merge_all, *mixed_rows],
        [shape((height, wide), F32), shape((height, wide), BF16)],
        flops=2 * height * wide * wide,
    )

    if direct:
        dense_far = [after(v, normed2) for v in (dense_x, dense_y, dense_xy)]
        dense_all = [dense_rows, *dense_far, dense_core] + [ctx_swap(v, 1) for v in dense_far]
    normed_all = tp_relay(normed2)
    normed_all[2] = after(normed_all[2], normed_all[1])
    picks = [[o for o in range(n_tp) if o % 4 in (0, 2)], [o for o in range(n_tp) if o % 4 in (1, 3)]]
    acts, pres, parts, mlps = ([None] * n_tp for _ in range(4))
    sums = []
    for pick in picks:
        count = len(pick)
        if sums:
            normed_all[3] = after(normed_all[3], sums[0])
        out = call(
            functools.partial(dense_kernel, count),
            "dense",
            None,
            [expand_add]
            + [normed_all[o] for o in pick]
            + [grad_rows[o] for o in pick]
            + dense_all,
            [shape((height, hidden_width), BF16)] * (2 * count)
            + [shape((height, wide), BF16)] * (2 * count)
            + [shape((1, hidden_width), F32)],
            flops=8 * count * height * wide * hidden_width,
        )
        for i, o in enumerate(pick):
            acts[o], pres[o], parts[o], mlps[o] = (out[j * count + i] for j in range(4))
        sums.append(out[-1])
    grad_parts = tp_exchange(parts)
    dense_outer = None
    if direct:
        (dense_outer,) = call(
            functools.partial(outer_kernel, order, [(n_tp, n_tp)] * 2),
            "dense_outer",
            place,
            [*normed_all, *pres, *grad_rows, *acts],
            [shape((group, 3 * block, hidden_width), BF16)],
            flops=4 * wide * hidden_width * q_len,
        )
        grad_parts[2] = after(grad_parts[2], dense_outer)
    (grad_near,) = call(
        add_kernel, "add", None, [grad_parts[0], grad_parts[2]], [shape((height, wide), F32)]
    )
    grad_parts = [grad_near] + [grad_parts[o] for o in range(1, n_tp) if o != 2]
    out = call(
        functools.partial(hidden_back_kernel, len(grad_parts), n_tp, order),
        "hidden_back",
        place,
        [grad_rows[0], hidden, wide_rows, merge_all, *grad_parts, *mixed_rows],
        [
            shape((height, wide), F32),
            shape((height, wide), BF16),
            shape((4, wide), F32),
        ]
        + [shape((height, width), BF16)] * n_tp,
        [pltpu.VMEM((group, block, wide), BF16), pltpu.SemaphoreType.DMA((group,))]
        if direct
        else [],
        flops=2 * height * wide * wide,
        whole=dense_outer,
    )
    if direct:
        dense_outer = out[-1]
        out = out[:-1]
    hidden_grad, grad_attn, four, grad_mixed = out[0], out[1], out[2], tp_exchange(out[3:])
    mlps = tp_exchange([mlps[0]] + [after(v, hidden_grad) for v in mlps[1:]])

    out = call(
        functools.partial(attend_back_kernel, heads, tile, tile, n_ctx, n_tp),
        "attention_back",
        limits,
        [lows, lse, query, *pairs, *mixed, *grad_mixed],
        [shape((q_len, width), BF16)] + [shape((q_len, 2 * width), BF16)] * n_ctx,
        attend_back_scratch(heads, tile, tile, q_len, width),
        flops=10 * q_len * q_len * n_ctx * width,
    )
    grad_query, grad_pairs = out[0], out[1:]
    joined = []
    for o in reversed(range(0, n_ctx, 2)):
        if joined:
            other = after(ctx_swap(grad_pairs[o + 1], 1), joined[-1])
            (total,) = call(
                join_kernel, "join", None, [other, grad_pairs[o]], [shape(other.shape, BF16)]
            )
        else:
            other = ctx_swap(after(grad_pairs[o + 1], *mlps), 1)
            total, layer_part = call(
                functools.partial(join_layer_kernel, order),
                "join_layer",
                place,
                [other, grad_pairs[o], hidden, wide_rows, *mlps],
                [shape(other.shape, BF16), shape((height, wide), BF16)],
            )
        joined.append(total)
    joined = joined[::-1]
    layer_parts = tp_relay(layer_part)
    joined = [joined[0]] + [ctx_swap(v, 2 * i) for i, v in enumerate(joined) if i]
    joined[-1] = after(joined[-1], layer_parts[1], layer_parts[2])
    out = call(
        functools.partial(project_back_kernel, span, order, len(joined), n_tp),
        "project_back",
        place,
        [normed1, grad_query, *joined, *first],
        [shape((height, wide), BF16)] * n_tp
        + [
            shape((q_len, 2 * width), BF16),
            shape((2, width), F32),
            shape((len(order), span, 3 * width), BF16),
        ],
        flops=12 * q_len * wide * width,
    )
    normed1_parts, (grad_pair, attend_sums, attend_outer) = out[:n_tp], out[n_tp:]
    (two,) = call(
        functools.partial(first_sums_kernel, order),
        "first_sums",
        place,
        [layer_input[0], *normed1_parts],
        [shape((2, wide), F32)],
    )
    normed1_parts = tp_exchange(normed1_parts)

    def placed(parts, outs=()):
        return call(
            functools.partial(place_kernel, n_tp, height),
            "place",
            place,
            parts,
            [shape((q_len, wide), BF16), *outs],
        )

    (layer_output,) = placed(layer_parts)

    def scattered(value):
        flat = jnp.reshape(value, (-1, value.shape[-1]))
        return lax.psum_scatter(flat, plane, scatter_dimension=0, tiled=True)

    if direct:
        attend_part = scattered(attend_outer)
        out = call(
            dense_total_kernel,
            "dense_total",
            None,
            [after(scattered(dense_outer), grad_pair)],
            [shape((block, hidden_width), F32), shape((hidden_width, block), F32)]
            + [shape((block, width), BF16)] * n_tp,
        )
        grad_expand, grad_shrink, merge_parts = out[0], out[1], out[2:]
        normed1_parts[-1] = after(normed1_parts[-1], grad_expand, two, layer_output)
    else:
        merge_parts = []
    low = block * width // wide if direct else 0
    input_parts = call(
        functools.partial(input_kernel, order, n_tp),
        "input_back",
        place,
        [input_rows, hidden_grad, wide_rows, *normed1_parts, *merge_parts],
        [shape((height + low, wide), BF16)] * n_tp,
    )
    input_part = input_parts[0]
    input_parts = tp_exchange(input_parts)

    if direct:
        (grad_attend,) = call(
            attend_total_kernel,
            "attend_total",
            None,
            [attend_part],
            [shape((3, block, width), F32)],
        )
        (small,) = call(
            functools.partial(small_kernel, order, head_block, n_tp),
            "small",
            place,
            [two, four, attend_sums, *sums],
            [shape((group * n_tp, 8, block), F32)],
        )
        table = call(
            functools.partial(small_total_kernel, n_tp),
            "small_total",
            place,
            [lax.all_to_all(after(small, input_part), ("dp", "ctx", "tp"), 0, 0)],
            [shape((1, block), F32)] * 7 + [shape((2, head_block), F32)],
        )
        rows = [jnp.reshape(v, (block,)) for v in table[:7]]
        expand_sum, attend_sum = rows[6], table[7]
        input_parts[-1] = after(input_parts[-1], grad_attend, *table)
        grad_attend = jnp.swapaxes(grad_attend, 0, 1)
    else:

        def cut(value, axis):
            return lax.psum_scatter(value, plane, scatter_dimension=axis, tiled=True)

        def outer_of(left, right):
            return cut(
                dot(jnp.concatenate(left), jnp.concatenate(right), 0, 0).astype(BF16), 0
            ).astype(F32)

        grad_expand = outer_of(normed_all, pres)
        grad_shrink = outer_of(grad_rows, acts).T
        grad_merge = outer_of([grad_attn], [jnp.concatenate(mixed_rows, axis=1)]).astype(BF16)
        grad_merge = [grad_merge[:, o * width : (o + 1) * width] for o in range(n_tp)]
        grad_merge = sum(v.astype(F32) for v in tp_exchange(grad_merge)).T
        grad_attend = jnp.reshape(cut(attend_outer[0], 0).astype(F32), (block, 3, width))
        table = lax.psum(cut(jnp.concatenate([two, four], axis=0), 1), "tp")
        rows = [table[i] for i in range(6)]
        expand_sum = cut(sum(sums)[0], 0)
        attend_sum = cut(attend_sums, 1)
    if direct:
        input_grad, grad_merge = placed(input_parts, [shape((width, block), F32)])
    else:
        (input_grad,) = placed(input_parts)
    return (
        layer_output[None],
        input_grad[None],
        rows[0],
        rows[1],
        grad_attend,
        attend_sum,
        grad_merge,
        rows[2],
        rows[3],
        rows[4],
        grad_expand,
        expand_sum,
        grad_shrink,
        rows[5],
    )


def solution(mesh):
    sizes = (mesh.shape["dp"], mesh.shape["ctx"], mesh.shape["tp"])
    return jax.shard_map(
        functools.partial(body, sizes),
        mesh=mesh,
        in_specs=(
            P("dp", "ctx", None),
            P("dp", "ctx", None),
            P("dp", None),
            P(("dp", "ctx")),
            P(("dp", "ctx")),
            P(("dp", "ctx"), None, "tp"),
            P(None, ("tp", "dp", "ctx")),
            P("tp", ("dp", "ctx")),
            P(("dp", "ctx")),
            P(("dp", "ctx")),
            P(("dp", "ctx")),
            P(("dp", "ctx"), "tp"),
            P(("tp", "dp", "ctx")),
            P("tp", ("dp", "ctx")),
            P(("dp", "ctx")),
        ),
        out_specs=(
            P("dp", "ctx", None),
            P("dp", "ctx", None),
            P(("dp", "ctx")),
            P(("dp", "ctx")),
            P(("dp", "ctx"), None, "tp"),
            P(None, ("tp", "dp", "ctx")),
            P("tp", ("dp", "ctx")),
            P(("dp", "ctx")),
            P(("dp", "ctx")),
            P(("dp", "ctx")),
            P(("dp", "ctx"), "tp"),
            P(("tp", "dp", "ctx")),
            P("tp", ("dp", "ctx")),
            P(("dp", "ctx")),
        ),
        check_vma=False,
    )
```

profile of v0, /device:TPU:0, one launch (start us, length us, event | category | flops | bytes accessed | tf_op | source)
XLA Modules:
  0.0 272.4 jit_solution(8035844702541741378)
XLA Ops:
  9.7 3.9 %collective-permute-start.2 = (bf16[136,768]{1,0:T(8,128)(2,1)}, bf16[136,768]{1,0:T(8,128)(2,1)S(1)}, u32[]{:S(2)}, u32[]{:S(2)}) collective-permute-start(bf16[136,768]{1,0:T(8,128)(2,1)} %pack.1.refs_0_.refs_2_), channel_id=1, source_target_pairs={{0,24},{4,28},{8,16},{12,20},{16,8},{20,12},{24,0},{28,4},{1,25},{... | collective-permute-start | bytes 626696 | tf_op jit(solution)/shard_map/ppermute | solution.py:674
  19.9 3.6 %collective-permute-done.1.refs_2_.refs_4_ = bf16[136,768]{1,0:T(8,128)(2,1)S(1)} collective-permute-done((bf16[136,768]{1,0:T(8,128)(2,1)}, bf16[136,768]{1,0:T(8,128)(2,1)S(1)}, u32[]{:S(2)}, u32[]{:S(2)}) %collective-permute-start.1) | collective-permute-done | bytes 208928 | tf_op jit(solution)/shard_map/ppermute | solution.py:674
  25.9 4.6 %project.1 = (bf16[512,1024]{1,0:T(8,128)(2,1)}, bf16[512,256]{1,0:T(8,128)(2,1)}, bf16[512,512]{1,0:T(8,128)(2,1)}, bf16[128,1024]{1,0:T(8,128)(2,1)}, f32[8,10...) custom-call(s32[3]{0:T(128)} %pad_add_fusion.scalars, bf16[512,1024]{1,0:T(8,128)(2,1)} %bitcast.34, ...), custom_call_target="tpu_custom_call" | custom-call | flops 805306368 | bytes 4855808 | tf_op jit(solution)/shard_map/project/pallas_call | solution.py:47
  34.8 2.4 order_grad.1
  37.2 9.4 %collective-permute-done.8.refs_2_ = bf16[512,512]{1,0:T(8,128)(2,1)S(1)} collective-permute-done((bf16[512,512]{1,0:T(8,128)(2,1)}, bf16[512,512]{1,0:T(8,128)(2,1)S(1)}, u32[]{:S(2)}, u32[]{:S(2)}) %collective-permute-start.8) | collective-permute-done | bytes 524320 | tf_op jit(solution)/shard_map/ppermute | solution.py:677
  51.3 5.3 %attention.1 = (bf16[128,256]{1,0:T(8,128)(2,1)}, bf16[128,256]{1,0:T(8,128)(2,1)}, bf16[128,256]{1,0:T(8,128)(2,1)}, bf16[128,256]{1,0:T(8,128)(2,1)}, f32[4,512]{1,0:T(4,128)}) custom-call(s32[5]{0:T(128)} %pad_add_fusion.1.scalars, s32[1,512]{1,0:T(1,128)} %bitcast.44, bf16[512,256]{1,0:T(8,128)(2,1)} %get-tuple-element.117.q_ref, ...), custom_call_target="tpu_custom_call" | custom-call | flops 1073741824 | bytes 2631680 | tf_op jit(solution)/shard_map/attention/pallas_call | solution.py:47
  58.2 2.6 collective-permute-start.13
  61.1 3.8 %collective-permute-done.13.refs_2_.refs_5_ = bf16[128,256]{1,0:T(8,128)(2,1)S(1)} collective-permute-done((bf16[128,256]{1,0:T(8,128)(2,1)}, bf16[128,256]{1,0:T(8,128)(2,1)S(1)}, u32[]{:S(2)}, u32[]{:S(2)}) %collective-permute-start.13) | collective-permute-done | bytes 65568 | tf_op jit(solution)/shard_map/ppermute | solution.py:680
  64.9 3.4 %collective-permute-done.14.refs_3_.refs_6_ = bf16[128,256]{1,0:T(8,128)(2,1)S(1)} collective-permute-done((bf16[128,256]{1,0:T(8,128)(2,1)}, bf16[128,256]{1,0:T(8,128)(2,1)S(1)}, u32[]{:S(2)}, u32[]{:S(2)}) %collective-permute-start.14) | collective-permute-done | bytes 65568 | tf_op jit(solution)/shard_map/ppermute | solution.py:680
  68.3 6.1 %all-gather.3.cloned.1.call-done = bf16[8192,128]{1,0:T(8,128)(2,1)} async-done(((bf16[256,128]{1,0:T(8,128)(2,1)}), bf16[8192,128]{1,0:T(8,128)(2,1)}) %all-gather.3.cloned.1.call-update) | async-done | bytes 2097168 | tf_op jit(solution)/shard_map/all_gather | solution.py:728
  74.5 3.2 %merge.1 = (f32[128,1024]{1,0:T(8,128)}, bf16[128,1024]{1,0:T(8,128)(2,1)}) custom-call(s32[3]{0:T(128)} %pad_add_fusion.scalars, bf16[128,1024]{1,0:T(8,128)(2,1)} %get-tuple-element.129.rows_ref, f32[8,1024]{1,0:T(8,128)} %get-tuple-element.130.wide_ref, bf16[8,4,256,128]{3,2,1,0:T(8,128)(2,1)} %bitcast.31, ...), custom_call_target="tpu_custom_call" | custom-call | flops 268435456 | bytes 3440640 | tf_op jit(solution)/shard_map/merge/pallas_call | solution.py:47
  82.0 11.7 %collective-permute-done.15.refs_1_.refs_2_ = bf16[128,1024]{1,0:T(8,128)(2,1)S(1)} collective-permute-done((bf16[128,1024]{1,0:T(8,128)(2,1)}, bf16[128,1024]{1,0:T(8,128)(2,1)S(1)}, u32[]{:S(2)}, u32[]{:S(2)}) %collective-permute-start.15) | collective-permute-done | bytes 262176 | tf_op jit(solution)/shard_map/ppermute | solution.py:680
  95.3 6.0 %dense.2 = (bf16[128,1024]{1,0:T(8,128)(2,1)}, bf16[128,1024]{1,0:T(8,128)(2,1)}, bf16[128,1024]{1,0:T(8,128)(2,1)}, bf16[128,1024]{1,0:T(8,128)(2,1)}, bf16[128...) custom-call(f32[1,1024]{1,0:T(1,128)} %get-tuple-element.132.expand_, ...), custom_call_target="tpu_custom_call" | custom-call | flops 2147483648 | bytes 7348224 | tf_op jit(solution)/shard_map/dense/pallas_call | solution.py:47
  101.4 3.3 %collective-permute-start.22 = (bf16[128,1024]{1,0:T(8,128)(2,1)}, bf16[128,1024]{1,0:T(8,128)(2,1)S(1)}, u32[]{:S(2)}, u32[]{:S(2)}) collective-permute-start(bf16[128,1024]{1,0:T(8,128)(2,1)} %get-tuple-element.141), channel_id=1, source_target_pairs={{0,2},{1,3},{2,0},{3,1},{4,6},{5,7},{6,4},{7,5},{8,10},{9,11},{10,... | collective-permute-start | bytes 786440 | tf_op jit(solution)/shard_map/ppermute | solution.py:680
  105.4 6.0 %dense.3 = (bf16[128,1024]{1,0:T(8,128)(2,1)}, bf16[128,1024]{1,0:T(8,128)(2,1)}, bf16[128,1024]{1,0:T(8,128)(2,1)}, bf16[128,1024]{1,0:T(8,128)(2,1)}, bf16[128...) custom-call(f32[1,1024]{1,0:T(1,128)} %get-tuple-element.132.expand_, ...), custom_call_target="tpu_custom_call" | custom-call | flops 2147483648 | bytes 7348224 | tf_op jit(solution)/shard_map/dense/pallas_call | solution.py:47
  112.8 7.1 %dense_outer.1.refs_7_ = bf16[8,384,1024]{2,1,0:T(8,128)(2,1)} custom-call(s32[3]{0:T(128)} %pad_add_fusion.scalars, bf16[128,1024]{1,0:T(8,128)(2,1)} %get-tuple-element.133.refs_0_, bf16[128,1024]{1,0:T(8,128)(2,1)} %copy-done.20, bf16[128,1024]{1,0:T(8,128)(2,1)} %copy-done.19, bf16[128,1024]{1,0:T(8,128)(2,1)} %copy-done.21, ...), custom_call_target="tpu_custom_call" | custom-call | flops 2147483648 | bytes 10485760 | tf_op jit(solution)/shard_map/dense_outer/pallas_call | solution.py:47
  122.6 5.2 %collective-permute-done.24.refs_1_ = bf16[128,1024]{1,0:T(8,128)(2,1)S(1)} collective-permute-done((bf16[128,1024]{1,0:T(8,128)(2,1)}, bf16[128,1024]{1,0:T(8,128)(2,1)S(1)}, u32[]{:S(2)}, u32[]{:S(2)}) %collective-permute-start.24) | collective-permute-done | bytes 262176 | tf_op jit(solution)/shard_map/ppermute | solution.py:680
  128.6 5.5 %hidden_back.1 = (f32[128,1024]{1,0:T(8,128)}, bf16[128,1024]{1,0:T(8,128)(2,1)}, f32[4,1024]{1,0:T(4,128)}, bf16[128,256]{1,0:T(8,128)(2,1)}, bf16[128,256]{1,0...) custom-call(s32[3]{0:T(128)} %pad_add_fusion.scalars, ...), custom_call_target="tpu_custom_call", output_to_operand_aliasing={{7}: (12, {})} | custom-call | flops 268435456 | bytes 5292032 | tf_op jit(solution)/shard_map/hidden_back/pallas_call | solution.py:47
  144.7 7.4 %attention_back.1 = (bf16[512,256]{1,0:T(8,128)(2,1)}, bf16[512,512]{1,0:T(8,128)(2,1)}, bf16[512,512]{1,0:T(8,128)(2,1)}, bf16[512,512]{1,0:T(8,128)(2,1)}, bf16[512,512]{1,0:T(8,128)(2,1)}) custom-call(s32[5]{0:T(128)} %pad_add_fusion.1.scalars, s32[1,512]{1,0:T(1,128)} %bitcast.45, f32[4,512]{1,0:T(4,128)} %get-tuple-element.124.lse_ref, ...), custom_call_target="tpu_custom_call" | custom-call | flops 2684354560 | bytes 5253120 | tf_op jit(solution)/shard_map/attention_back/pallas_call | solution.py:47
  153.1 9.2 %collective-permute-done.30.refs_2_ = bf16[128,1024]{1,0:T(8,128)(2,1)S(1)} collective-permute-done((bf16[128,1024]{1,0:T(8,128)(2,1)S(1)}, bf16[128,1024]{1,0:T(8,128)(2,1)S(1)}, u32[]{:S(2)}, u32[]{:S(2)}) %collective-permute-start.30) | collective-permute-done | bytes 262176 | tf_op jit(solution)/shard_map/ppermute | solution.py:680
  165.3 3.0 %join_layer.1 = (bf16[512,512]{1,0:T(8,128)(2,1)}, bf16[128,1024]{1,0:T(8,128)(2,1)}) custom-call(s32[3]{0:T(128)} %pad_add_fusion.scalars, bf16[512,512]{1,0:T(8,128)(2,1)} %copy-done.2, bf16[512,512]{1,0:T(8,128)(2,1)} %get-tuple-element.171.right_ref, f32[128,1024]{1,0:T(8,128)} %get-tuple-element.131.hidden_ref, f32[8,1024]{1,0:T(8,128)} %get-tuple-element.130.wide_ref, ...), custom_call_target="tpu_custom_call" | custom-call | bytes 3440640 | tf_op jit(solution)/shard_map/join_layer/pallas_call | solution.py:47
  170.3 5.6 %collective-permute-start.34 = (bf16[128,1024]{1,0:T(8,128)(2,1)}, bf16[128,1024]{1,0:T(8,128)(2,1)S(1)}, u32[]{:S(2)}, u32[]{:S(2)}) collective-permute-start(bf16[128,1024]{1,0:T(8,128)(2,1)} %get-tuple-element.172.refs_0_), channel_id=1, source_target_pairs={{0,2},{1,3},{2,0},{3,1},{4,6},{5,7},{6,4},{7,5},{8,10},{9,11},{10,... | collective-permute-start | bytes 786440 | tf_op jit(solution)/shard_map/ppermute | solution.py:680
  178.8 9.3 %collective-permute-done.34.refs_2_ = bf16[128,1024]{1,0:T(8,128)(2,1)S(1)} collective-permute-done((bf16[128,1024]{1,0:T(8,128)(2,1)}, bf16[128,1024]{1,0:T(8,128)(2,1)S(1)}, u32[]{:S(2)}, u32[]{:S(2)}) %collective-permute-start.34) | collective-permute-done | bytes 262176 | tf_op jit(solution)/shard_map/ppermute | solution.py:680
  189.0 6.5 %project_back.1 = (bf16[128,1024]{1,0:T(8,128)(2,1)}, bf16[128,1024]{1,0:T(8,128)(2,1)}, bf16[128,1024]{1,0:T(8,128)(2,1)}, bf16[128,1024]{1,0:T(8,128)(2,1)}, b...) custom-call(s32[3]{0:T(128)} %pad_add_fusion.scalars, ...), custom_call_target="tpu_custom_call" | custom-call | flops 1610612736 | bytes 7178240 | tf_op jit(solution)/shard_map/project_back/pallas_call | solution.py:47
  201.7 3.3 %first_sums.1.two_ref = f32[2,1024]{1,0:T(2,128)} custom-call(s32[3]{0:T(128)} %pad_add_fusion.scalars, bf16[512,1024]{1,0:T(8,128)(2,1)} %bitcast.35, bf16[128,1024]{1,0:T(8,128)(2,1)} %get-tuple-element.180.refs_0_, bf16[128,1024]{1,0:T(8,128)(2,1)} %get-tuple-element.181.refs_1_, bf16[128,1024]{1,0:T(8,128)(2,1)} %get-tuple-element.182.refs_2_, ...), custom_call_target="tpu_custom_call" | custom-call | bytes 2105344 | tf_op jit(solution)/shard_map/first_sums/pallas_call | solution.py:47
  212.3 8.2 %collective-permute-done.38.refs_1_ = bf16[128,1024]{1,0:T(8,128)(2,1)S(1)} collective-permute-done((bf16[128,1024]{1,0:T(8,128)(2,1)}, bf16[128,1024]{1,0:T(8,128)(2,1)S(1)}, u32[]{:S(2)}, u32[]{:S(2)}) %collective-permute-start.38) | collective-permute-done | bytes 262176 | tf_op jit(solution)/shard_map/ppermute | solution.py:680
  223.4 3.3 %input_back.1 = (bf16[160,1024]{1,0:T(8,128)(2,1)}, bf16[160,1024]{1,0:T(8,128)(2,1)}, bf16[160,1024]{1,0:T(8,128)(2,1)}, bf16[160,1024]{1,0:T(8,128)(2,1)}) custom-call(s32[3]{0:T(128)} %pad_add_fusion.scalars, bf16[128,1024]{1,0:T(8,128)(2,1)} %get-tuple-element.129.rows_ref, f32[128,1024]{1,0:T(8,128)} %get-tuple-element.164.back_ref, ...), custom_call_target="tpu_custom_call" | custom-call | bytes 3440640 | tf_op jit(solution)/shard_map/input_back/pallas_call | solution.py:47
  226.7 2.6 collective-permute-start.43
  232.8 3.9 %all-to-all-start = ((f32[32,8,128]{2,1,0:T(8,128)}), f32[32,8,128]{2,1,0:T(8,128)S(1)}, u32[]{:S(2)}, u32[]{:S(2)}) async-start(f32[32,8,128]{2,1,0:T(8,128)} %small.1), calls=%async_computation.2 | async-start | bytes 262144 | tf_op jit(solution)/shard_map/all_to_all | solution.py:991
  236.7 9.1 %reduce-scatter.5.cloned.1.call-done.in_ref = bf16[128,768]{1,0:T(8,128)(2,1)} async-done(((bf16[1024,768]{1,0:T(8,128)(2,1)}), bf16[128,768]{1,0:T(8,128)(2,1)}) %reduce-scatter.5.cloned.1.call-update) | async-done | bytes 196624 | tf_op jit(solution)/shard_map/reduce_scatter | solution.py:945
  247.4 12.1 %all-to-all-done.in_ref = f32[32,8,128]{2,1,0:T(8,128)S(1)} async-done(((f32[32,8,128]{2,1,0:T(8,128)}), f32[32,8,128]{2,1,0:T(8,128)S(1)}, u32[]{:S(2)}, u32[]{:S(2)}) %all-to-all-start) | async-done | bytes 131104 | tf_op jit(solution)/shard_map/all_to_all | solution.py:991
  263.3 2.6 place.3
  (199 shorter events, 79.0 us)
Async XLA Ops:
  7.2 67.3 %all-gather.3.cloned.1.call-start = ((), (), s32[]{:S(2)}) async-start(), calls=%async_computation.5 | async-start | bytes 2162688 | tf_op jit(solution)/shard_map/all_gather | solution.py:728
  7.9 200.0 %reduce-scatter.3.cloned.1.call-start = ((), (), s32[]{:S(2)}) async-start(), calls=%async_computation.3 | async-start | bytes 7077888 | tf_op jit(solution)/shard_map/reduce_scatter | solution.py:945
  9.7 10.1 %collective-permute-start.2 = (bf16[136,768]{1,0:T(8,128)(2,1)}, bf16[136,768]{1,0:T(8,128)(2,1)S(1)}, u32[]{:S(2)}, u32[]{:S(2)}) collective-permute-start(bf16[136,768]{1,0:T(8,128)(2,1)} %pack.1.refs_0_.refs_2_), channel_id=1, source_target_pairs={{0,24},{4,28},{8,16},{12,20},{16,8},{20,12},{24,0},{28,4},{1,25},{... | collective-permute-start | bytes 626696 | tf_op jit(solution)/shard_map/ppermute | solution.py:674
  30.5 16.1 %collective-permute-start.8 = (bf16[512,512]{1,0:T(8,128)(2,1)}, bf16[512,512]{1,0:T(8,128)(2,1)S(1)}, u32[]{:S(2)}, u32[]{:S(2)}) collective-permute-start(bf16[512,512]{1,0:T(8,128)(2,1)} %get-tuple-element.118.refs_0_), channel_id=1, source_target_pairs={{0,8},{4,12},{8,0},{12,4},{1,9},{5,13},{9,1},{13,5},{2,10},{6,14},... | collective-permute-start | bytes 1572872 | tf_op jit(solution)/shard_map/ppermute | solution.py:677
  34.2 14.7 %collective-permute-start.11 = (bf16[256,1024]{1,0:T(8,128)(2,1)}, bf16[256,1024]{1,0:T(8,128)(2,1)S(1)}, u32[]{:S(2)}, u32[]{:S(2)}) collective-permute-start(bf16[256,1024]{1,0:T(8,128)(2,1)} %turn.1.refs_4_), channel_id=1, source_target_pairs={{0,4},{4,0},{8,12},{12,8},{1,5},{5,1},{9,13},{13,9},{2,6},{6,2},{1... | collective-permute-start | bytes 1572872 | tf_op jit(solution)/shard_map/ppermute | solution.py:677
  34.2 16.1 %collective-permute-start.10 = (bf16[256,1024]{1,0:T(8,128)(2,1)}, bf16[256,1024]{1,0:T(8,128)(2,1)S(1)}, u32[]{:S(2)}, u32[]{:S(2)}) collective-permute-start(bf16[256,1024]{1,0:T(8,128)(2,1)} %turn.1.refs_4_), channel_id=1, source_target_pairs={{0,16},{4,20},{8,24},{12,28},{16,0},{20,4},{24,8},{28,12},{1,17},{... | collective-permute-start | bytes 1572872 | tf_op jit(solution)/shard_map/ppermute | solution.py:674
  47.2 30.5 %collective-permute-start.18 = (bf16[256,1024]{1,0:T(8,128)(2,1)}, bf16[256,1024]{1,0:T(8,128)(2,1)S(1)}, u32[]{:S(2)}, u32[]{:S(2)}) collective-permute-start(bf16[256,1024]{1,0:T(8,128)(2,1)} %turn.1.refs_4_), channel_id=1, source_target_pairs={{0,24},{4,28},{8,16},{12,20},{16,8},{20,12},{24,0},{28,4},{1,25},{... | collective-permute-start | bytes 1572872 | tf_op jit(solution)/shard_map/ppermute | solution.py:674
  48.9 28.8 %collective-permute-start.17 = (bf16[256,1024]{1,0:T(8,128)(2,1)}, bf16[256,1024]{1,0:T(8,128)(2,1)}, u32[]{:S(2)}, u32[]{:S(2)}) collective-permute-start(bf16[256,1024]{1,0:T(8,128)(2,1)} %turn.1.refs_4_), channel_id=1, source_target_pairs={{0,8},{4,12},{8,0},{12,4},{16,24},{20,28},{24,16},{28,20},{1,9},{5... | collective-permute-start | bytes 1572872 | tf_op jit(solution)/shard_map/ppermute | solution.py:674
  77.7 16.4 %collective-permute-start.19 = (bf16[256,1024]{1,0:T(8,128)(2,1)}, bf16[256,1024]{1,0:T(8,128)(2,1)S(1)}, u32[]{:S(2)}, u32[]{:S(2)}) collective-permute-start(bf16[256,1024]{1,0:T(8,128)(2,1)} %collective-permute-done.17.refs_5_), channel_id=1, source_target_pairs={{0,4},{4,0},{8,12},{12,8},{1,5},{5,1},{9,13},{13,9},{2,6},{6,2},{1... | collective-permute-start | bytes 1572872 | tf_op jit(solution)/shard_map/ppermute | solution.py:677
  78.0 16.1 %collective-permute-start.20 = (bf16[256,1024]{1,0:T(8,128)(2,1)S(1)}, bf16[256,1024]{1,0:T(8,128)(2,1)S(1)}, u32[]{:S(2)}, u32[]{:S(2)}) collective-permute-start(bf16[256,1024]{1,0:T(8,128)(2,1)S(1)} %collective-permute-done.10.refs_6_), channel_id=1, source_target_pairs={{0,4},{4,0},{8,12},{12,8},{1,5},{5,1},{9,13},{13,9},{2,6},{6,2},{1... | collective-permute-start | bytes 1572872 | tf_op jit(solution)/shard_map/ppermute | solution.py:677
  78.2 15.9 %collective-permute-start.21 = (bf16[256,1024]{1,0:T(8,128)(2,1)S(1)}, bf16[256,1024]{1,0:T(8,128)(2,1)S(1)}, u32[]{:S(2)}, u32[]{:S(2)}) collective-permute-start(bf16[256,1024]{1,0:T(8,128)(2,1)S(1)} %collective-permute-done.18.refs_7_), channel_id=1, source_target_pairs={{0,4},{4,0},{8,12},{12,8},{1,5},{5,1},{9,13},{13,9},{2,6},{6,2},{1... | collective-permute-start | bytes 1572872 | tf_op jit(solution)/shard_map/ppermute | solution.py:677
  78.5 15.3 %collective-permute-start.15 = (bf16[128,1024]{1,0:T(8,128)(2,1)}, bf16[128,1024]{1,0:T(8,128)(2,1)S(1)}, u32[]{:S(2)}, u32[]{:S(2)}) collective-permute-start(bf16[128,1024]{1,0:T(8,128)(2,1)} %get-tuple-element.133.refs_0_), channel_id=1, source_target_pairs={{0,2},{1,3},{2,0},{3,1},{4,6},{5,7},{6,4},{7,5},{8,10},{9,11},{10,... | collective-permute-start | bytes 786440 | tf_op jit(solution)/shard_map/ppermute | solution.py:680
  80.5 13.6 %collective-permute-start.16 = (bf16[128,1024]{1,0:T(8,128)(2,1)}, bf16[128,1024]{1,0:T(8,128)(2,1)S(1)}, u32[]{:S(2)}, u32[]{:S(2)}) collective-permute-start(bf16[128,1024]{1,0:T(8,128)(2,1)} %get-tuple-element.133.refs_0_), channel_id=1, source_target_pairs={{0,1},{1,0},{2,3},{3,2},{4,5},{5,4},{6,7},{7,6},{8,9},{9,8},{10,11... | collective-permute-start | bytes 786440 | tf_op jit(solution)/shard_map/ppermute | solution.py:680
  93.8 10.8 %collective-permute-start.23 = (bf16[128,1024]{1,0:T(8,128)(2,1)S(1)}, bf16[128,1024]{1,0:T(8,128)(2,1)S(1)}, u32[]{:S(2)}, u32[]{:S(2)}) collective-permute-start(bf16[128,1024]{1,0:T(8,128)(2,1)S(1)} %collective-permute-done.15.refs_1_.refs_2_), channel_id=1, source_target_pairs={{0,1},{1,0},{2,3},{3,2},{4,5},{5,4},{6,7},{7,6},{8,9},{9,8},{10,11... | collective-permute-start | bytes 786440 | tf_op jit(solution)/shard_map/ppermute | solution.py:680
  101.4 18.6 %collective-permute-start.22 = (bf16[128,1024]{1,0:T(8,128)(2,1)}, bf16[128,1024]{1,0:T(8,128)(2,1)S(1)}, u32[]{:S(2)}, u32[]{:S(2)}) collective-permute-start(bf16[128,1024]{1,0:T(8,128)(2,1)} %get-tuple-element.141), channel_id=1, source_target_pairs={{0,2},{1,3},{2,0},{3,1},{4,6},{5,7},{6,4},{7,5},{8,10},{9,11},{10,... | collective-permute-start | bytes 786440 | tf_op jit(solution)/shard_map/ppermute | solution.py:680
  111.4 16.4 %collective-permute-start.24 = (bf16[128,1024]{1,0:T(8,128)(2,1)}, bf16[128,1024]{1,0:T(8,128)(2,1)S(1)}, u32[]{:S(2)}, u32[]{:S(2)}) collective-permute-start(bf16[128,1024]{1,0:T(8,128)(2,1)} %get-tuple-element.155), channel_id=1, source_target_pairs={{0,1},{1,0},{2,3},{3,2},{4,5},{5,4},{6,7},{7,6},{8,9},{9,8},{10,11... | collective-permute-start | bytes 786440 | tf_op jit(solution)/shard_map/ppermute | solution.py:680
  111.4 16.4 %collective-permute-start.25 = (bf16[128,1024]{1,0:T(8,128)(2,1)}, bf16[128,1024]{1,0:T(8,128)(2,1)S(1)}, u32[]{:S(2)}, u32[]{:S(2)}) collective-permute-start(bf16[128,1024]{1,0:T(8,128)(2,1)} %get-tuple-element.156), channel_id=1, source_target_pairs={{0,3},{1,2},{2,1},{3,0},{4,7},{5,6},{6,5},{7,4},{8,11},{9,10},{10,... | collective-permute-start | bytes 786440 | tf_op jit(solution)/shard_map/ppermute | solution.py:680
  134.2 111.5 %reduce-scatter.5.cloned.1.call-start = ((), (), s32[]{:S(2)}) async-start(), calls=%async_computation.4 | async-start | bytes 1769472 | tf_op jit(solution)/shard_map/reduce_scatter | solution.py:945
  139.3 13.7 %collective-permute-start.29 = (bf16[128,1024]{1,0:T(8,128)(2,1)S(1)}, bf16[128,1024]{1,0:T(8,128)(2,1)S(1)}, u32[]{:S(2)}, u32[]{:S(2)}) collective-permute-start(bf16[128,1024]{1,0:T(8,128)(2,1)S(1)} %copy-done.37), channel_id=1, source_target_pairs={{0,1},{1,0},{2,3},{3,2},{4,5},{5,4},{6,7},{7,6},{8,9},{9,8},{10,11... | collective-permute-start | bytes 786440 | tf_op jit(solution)/shard_map/ppermute | solution.py:680
  139.3 22.9 %collective-permute-start.30 = (bf16[128,1024]{1,0:T(8,128)(2,1)S(1)}, bf16[128,1024]{1,0:T(8,128)(2,1)S(1)}, u32[]{:S(2)}, u32[]{:S(2)}) collective-permute-start(bf16[128,1024]{1,0:T(8,128)(2,1)S(1)} %copy-done.35), channel_id=1, source_target_pairs={{0,2},{1,3},{2,0},{3,1},{4,6},{5,7},{6,4},{7,5},{8,10},{9,11},{10,... | collective-permute-start | bytes 786440 | tf_op jit(solution)/shard_map/ppermute | solution.py:680
  141.6 20.7 %collective-permute-start.31 = (bf16[128,1024]{1,0:T(8,128)(2,1)S(1)}, bf16[128,1024]{1,0:T(8,128)(2,1)S(1)}, u32[]{:S(2)}, u32[]{:S(2)}) collective-permute-start(bf16[128,1024]{1,0:T(8,128)(2,1)S(1)} %copy-done.36), channel_id=1, source_target_pairs={{0,3},{1,2},{2,1},{3,0},{4,7},{5,6},{6,5},{7,4},{8,11},{9,10},{10,... | collective-permute-start | bytes 786440 | tf_op jit(solution)/shard_map/ppermute | solution.py:680
  162.4 13.5 %collective-permute-start.36 = (bf16[512,512]{1,0:T(8,128)(2,1)}, bf16[512,512]{1,0:T(8,128)(2,1)S(1)}, u32[]{:S(2)}, u32[]{:S(2)}) collective-permute-start(bf16[512,512]{1,0:T(8,128)(2,1)} %get-tuple-element.175), channel_id=1, source_target_pairs={{0,4},{4,0},{8,12},{12,8},{1,5},{5,1},{9,13},{13,9},{2,6},{6,2},{1... | collective-permute-start | bytes 1572872 | tf_op jit(solution)/shard_map/ppermute | solution.py:677
  168.3 20.0 %collective-permute-start.37 = (bf16[512,512]{1,0:T(8,128)(2,1)}, bf16[512,512]{1,0:T(8,128)(2,1)S(1)}, u32[]{:S(2)}, u32[]{:S(2)}) collective-permute-start(bf16[512,512]{1,0:T(8,128)(2,1)} %get-tuple-element.176), channel_id=1, source_target_pairs={{0,8},{4,12},{8,0},{12,4},{1,9},{5,13},{9,1},{13,5},{2,10},{6,14},... | collective-permute-start | bytes 1572872 | tf_op jit(solution)/shard_map/ppermute | solution.py:677
  170.3 17.8 %collective-permute-start.34 = (bf16[128,1024]{1,0:T(8,128)(2,1)}, bf16[128,1024]{1,0:T(8,128)(2,1)S(1)}, u32[]{:S(2)}, u32[]{:S(2)}) collective-permute-start(bf16[128,1024]{1,0:T(8,128)(2,1)} %get-tuple-element.172.refs_0_), channel_id=1, source_target_pairs={{0,2},{1,3},{2,0},{3,1},{4,6},{5,7},{6,4},{7,5},{8,10},{9,11},{10,... | collective-permute-start | bytes 786440 | tf_op jit(solution)/shard_map/ppermute | solution.py:680
  175.9 12.2 %collective-permute-start.33 = (bf16[128,1024]{1,0:T(8,128)(2,1)}, bf16[128,1024]{1,0:T(8,128)(2,1)S(1)}, u32[]{:S(2)}, u32[]{:S(2)}) collective-permute-start(bf16[128,1024]{1,0:T(8,128)(2,1)} %get-tuple-element.172.refs_0_), channel_id=1, source_target_pairs={{0,1},{1,0},{2,3},{3,2},{4,5},{5,4},{6,7},{7,6},{8,9},{9,8},{10,11... | collective-permute-start | bytes 786440 | tf_op jit(solution)/shard_map/ppermute | solution.py:680
  197.3 15.1 %collective-permute-start.40 = (bf16[128,1024]{1,0:T(8,128)(2,1)}, bf16[128,1024]{1,0:T(8,128)(2,1)S(1)}, u32[]{:S(2)}, u32[]{:S(2)}) collective-permute-start(bf16[128,1024]{1,0:T(8,128)(2,1)} %get-tuple-element.183.refs_3_), channel_id=1, source_target_pairs={{0,3},{1,2},{2,1},{3,0},{4,7},{5,6},{6,5},{7,4},{8,11},{9,10},{10,... | collective-permute-start | bytes 786440 | tf_op jit(solution)/shard_map/ppermute | solution.py:680
  199.5 21.0 %collective-permute-start.38 = (bf16[128,1024]{1,0:T(8,128)(2,1)}, bf16[128,1024]{1,0:T(8,128)(2,1)S(1)}, u32[]{:S(2)}, u32[]{:S(2)}) collective-permute-start(bf16[128,1024]{1,0:T(8,128)(2,1)} %get-tuple-element.181.refs_1_), channel_id=1, source_target_pairs={{0,1},{1,0},{2,3},{3,2},{4,5},{5,4},{6,7},{7,6},{8,9},{9,8},{10,11... | collective-permute-start | bytes 786440 | tf_op jit(solution)/shard_map/ppermute | solution.py:680
  200.1 22.6 %collective-permute-start.39 = (bf16[128,1024]{1,0:T(8,128)(2,1)}, bf16[128,1024]{1,0:T(8,128)(2,1)S(1)}, u32[]{:S(2)}, u32[]{:S(2)}) collective-permute-start(bf16[128,1024]{1,0:T(8,128)(2,1)} %get-tuple-element.182.refs_2_), channel_id=1, source_target_pairs={{0,2},{1,3},{2,0},{3,1},{4,6},{5,7},{6,4},{7,5},{8,10},{9,11},{10,... | collective-permute-start | bytes 786440 | tf_op jit(solution)/shard_map/ppermute | solution.py:680
  226.7 35.0 %collective-permute-start.43 = (bf16[160,1024]{1,0:T(8,128)(2,1)}, bf16[160,1024]{1,0:T(8,128)(2,1)S(1)}, u32[]{:S(2)}, u32[]{:S(2)}) collective-permute-start(bf16[160,1024]{1,0:T(8,128)(2,1)} %get-tuple-element.194), channel_id=1, source_target_pairs={{0,3},{1,2},{2,1},{3,0},{4,7},{5,6},{6,5},{7,4},{8,11},{9,10},{10,... | collective-permute-start | bytes 983048 | tf_op jit(solution)/shard_map/ppermute | solution.py:680
  229.4 32.4 %collective-permute-start.41 = (bf16[160,1024]{1,0:T(8,128)(2,1)}, bf16[160,1024]{1,0:T(8,128)(2,1)S(1)}, u32[]{:S(2)}, u32[]{:S(2)}) collective-permute-start(bf16[160,1024]{1,0:T(8,128)(2,1)} %get-tuple-element.192), channel_id=1, source_target_pairs={{0,1},{1,0},{2,3},{3,2},{4,5},{5,4},{6,7},{7,6},{8,9},{9,8},{10,11... | collective-permute-start | bytes 983048 | tf_op jit(solution)/shard_map/ppermute | solution.py:680
  229.4 32.4 %collective-permute-start.42 = (bf16[160,1024]{1,0:T(8,128)(2,1)}, bf16[160,1024]{1,0:T(8,128)(2,1)S(1)}, u32[]{:S(2)}, u32[]{:S(2)}) collective-permute-start(bf16[160,1024]{1,0:T(8,128)(2,1)} %get-tuple-element.193), channel_id=1, source_target_pairs={{0,2},{1,3},{2,0},{3,1},{4,6},{5,7},{6,4},{7,5},{8,10},{9,11},{10,... | collective-permute-start | bytes 983048 | tf_op jit(solution)/shard_map/ppermute | solution.py:680
  232.8 26.8 %all-to-all-start = ((f32[32,8,128]{2,1,0:T(8,128)}), f32[32,8,128]{2,1,0:T(8,128)S(1)}, u32[]{:S(2)}, u32[]{:S(2)}) async-start(f32[32,8,128]{2,1,0:T(8,128)} %small.1), calls=%async_computation.2 | async-start | bytes 262144 | tf_op jit(solution)/shard_map/all_to_all | solution.py:991
  (67 other events, 392.9 us)
Sparse Core Ops, SparseCore 0:
  10.9 63.4 all-gather.2
  134.3 69.0 reduce-scatter.2
  207.0 38.6 reduce-scatter.4
where the time goes:
time: 273 us; the launch traced here: 272 us
  waiting for transfers between devices  103 us (38%)
  Pallas kernels  83.3 us (31%)
  starting transfers between devices  56 us (21%)
  between operations  14.1 us (5%)
  local copies, waits for them, and re-layouts  13.9 us (5%)
    pallas_call x23, Pallas kernels, call(): pl.pallas_call(kernel, grid=(1,), out_shape=tuple(outs), in_specs=[pl.Blo...  83.3 us
    ppermute x24, waiting for transfers between devices, tp_swap(): return lax.ppermute(value, 'tp', [(i, i ^ offset) for i in range(n_tp)])  56.6 us
    ppermute x24, starting transfers between devices, tp_swap(): return lax.ppermute(value, 'tp', [(i, i ^ offset) for i in range(n_tp)])  37.9 us
    unnamed x102, local copies, waits for them, and re-layouts  12.4 us
    all_to_all x1, waiting for transfers between devices, body(): lax.all_to_all(after(small, input_part), ('dp', 'ctx', 'tp'), 0, 0)  12.1 us
    ppermute x14, waiting for transfers between devices, ctx_swap(): return lax.ppermute(value, 'ctx', [(i, i ^ offset) for i in range(n_ctx)])  11.9 us
    reduce_scatter x2, waiting for transfers between devices, scattered(): return lax.psum_scatter(flat, plane, scatter_dimension=0, tiled=True)  9.05 us
    ppermute x6, starting transfers between devices, plane_swap(): return lax.ppermute(value, plane, [(i, i ^ offset) for i in range(group)])  8.24 us
  transfers between devices with their start and end apart: 48, of which 23 were waited for; matrix products, arithmetic and copies ran while one was open for 1% of the time, Pallas kernels for 28%

commit v1 on v0

--- a/solution.py
+++ b/solution.py
@@ -9,6 +9,17 @@
 
 HD = 64
 NEG = -1e30
+ROOMY = (
+    "dense",
+    "dense_outer",
+    "add",
+    "join_layer",
+    "join",
+    "first_sums",
+    "dense_total",
+    "input_back",
+    "place",
+)
 F32 = jnp.float32
 BF16 = jnp.bfloat16
 
@@ -52,7 +63,7 @@
         out_specs=tuple(out_specs),
         input_output_aliases=alias,
         scratch_shapes=list(scratch),
-        compiler_params=pltpu.CompilerParams(vmem_limit_bytes=56 << 20),
+        compiler_params=pltpu.CompilerParams(vmem_limit_bytes=(24 if name in ROOMY else 56) << 20),
         cost_estimate=pl.CostEstimate(
             flops=flops, transcendentals=0, bytes_accessed=moved
         ),
@@ -984,16 +995,21 @@
             [two, four, attend_sums, *sums],
             [shape((group * n_tp, 8, block), F32)],
         )
+        input_parts[-1] = after(input_parts[-1], grad_attend)
+        input_grad, grad_merge = placed(input_parts, [shape((width, block), F32)])
         table = call(
             functools.partial(small_total_kernel, n_tp),
             "small_total",
             place,
-            [lax.all_to_all(after(small, input_part), ("dp", "ctx", "tp"), 0, 0)],
+            [
+                after(
+                    lax.all_to_all(after(small, input_part), ("dp", "ctx", "tp"), 0, 0), input_grad
+                )
+            ],
             [shape((1, block), F32)] * 7 + [shape((2, head_block), F32)],
         )
         rows = [jnp.reshape(v, (block,)) for v in table[:7]]
         expand_sum, attend_sum = rows[6], table[7]
-        input_parts[-1] = after(input_parts[-1], grad_attend, *table)
         grad_attend = jnp.swapaxes(grad_attend, 0, 1)
     else:
 
@@ -1011,14 +1027,11 @@
         grad_merge = [grad_merge[:, o * width : (o + 1) * width] for o in range(n_tp)]
         grad_merge = sum(v.astype(F32) for v in tp_exchange(grad_merge)).T
         grad_attend = jnp.reshape(cut(attend_outer[0], 0).astype(F32), (block, 3, width))
+        (input_grad,) = placed(input_parts)
         table = lax.psum(cut(jnp.concatenate([two, four], axis=0), 1), "tp")
         rows = [table[i] for i in range(6)]
         expand_sum = cut(sum(sums)[0], 0)
         attend_sum = cut(attend_sums, 1)
-    if direct:
-        input_grad, grad_merge = placed(input_parts, [shape((width, block), F32)])
-    else:
-        (input_grad,) = placed(input_parts)
     return (
         layer_output[None],
         input_grad[None],

time: 273 us -> 262 us (0.960)
  Pallas kernels: 83.3 us -> 61.1 us
  local copies, waits for them, and re-layouts: 13.9 us -> 20.3 us
    pallas_call x23, Pallas kernels: 83.3 us -> 61.1 us  [call(): pl.pallas_call(kernel, grid=(1,), out_shape=tuple(outs), in_specs=[pl.Blo...]
    all_to_all x1, waiting for transfers between devices: 12.1 us -> 0.01 us  [body(): lax.all_to_all(after(small, input_part), ('dp', 'ctx', 'tp'), 0, 0)]
    ppermute x24, waiting for transfers between devices: 56.6 us -> 65.2 us  [tp_swap(): return lax.ppermute(value, 'tp', [(i, i ^ offset) for i in range(n_tp)])]
    unnamed x102 -> x122, local copies, waits for them, and re-layouts: 12.4 us -> 18.8 us
    ppermute x24, starting transfers between devices: 37.9 us -> 41.7 us  [tp_swap(): return lax.ppermute(value, 'tp', [(i, i ^ offset) for i in range(n_tp)])]
    reduce_scatter x2, waiting for transfers between devices: 9.05 us -> 12.8 us  [scattered(): return lax.psum_scatter(flat, plane, scatter_dimension=0, tiled=True)]
  transfers between devices with their start and end apart: 48 -> 48, of which waited for: 23 -> 23; matrix products, arithmetic and copies ran while one was open for 1% -> 2% of each run, Pallas kernels for 28% -> 21%
where the time goes in v1:
time: 262 us; the launch traced here: 261 us
  waiting for transfers between devices  105 us (40%)
  Pallas kernels  61.1 us (23%)
  starting transfers between devices  58.4 us (22%)
  local copies, waits for them, and re-layouts  20.3 us (8%)
  between operations  14.2 us (5%)
    ppermute x24, waiting for transfers between devices, tp_swap(): return lax.ppermute(value, 'tp', [(i, i ^ offset) for i in range(n_tp)])  65.2 us
    pallas_call x23, Pallas kernels, call(): pl.pallas_call(kernel, grid=(1,), out_shape=tuple(outs), in_specs=[pl.Blo...  61.1 us
    ppermute x24, starting transfers between devices, tp_swap(): return lax.ppermute(value, 'tp', [(i, i ^ offset) for i in range(n_tp)])  41.7 us
    unnamed x122, local copies, waits for them, and re-layouts  18.8 us
    ppermute x14, waiting for transfers between devices, ctx_swap(): return lax.ppermute(value, 'ctx', [(i, i ^ offset) for i in range(n_ctx)])  13.8 us
    reduce_scatter x2, waiting for transfers between devices, scattered(): return lax.psum_scatter(flat, plane, scatter_dimension=0, tiled=True)  12.8 us
    ppermute x6, starting transfers between devices, plane_swap(): return lax.ppermute(value, plane, [(i, i ^ offset) for i in range(group)])  8.25 us
    ppermute x6, waiting for transfers between devices, plane_swap(): return lax.ppermute(value, plane, [(i, i ^ offset) for i in range(group)])  6.12 us
  transfers between devices with their start and end apart: 48, of which 23 were waited for; matrix products, arithmetic and copies ran while one was open for 2% of the time, Pallas kernels for 21%

profile of v1, /device:TPU:0, one launch (start us, length us, event | category | flops | bytes accessed | tf_op | source)
XLA Modules:
  0.0 261.2 jit_solution(13140671918264398166)
XLA Ops:
  9.7 3.9 %collective-permute-start.2 = (bf16[136,768]{1,0:T(8,128)(2,1)}, bf16[136,768]{1,0:T(8,128)(2,1)S(1)}, u32[]{:S(2)}, u32[]{:S(2)}) collective-permute-start(bf16[136,768]{1,0:T(8,128)(2,1)} %pack.1.refs_0_.refs_2_), channel_id=1, source_target_pairs={{0,24},{4,28},{8,16},{12,20},{16,8},{20,12},{24,0},{28,4},{1,25},{... | collective-permute-start | bytes 626696 | tf_op jit(solution)/shard_map/ppermute | solution.py:685
  19.9 3.6 %collective-permute-done.1.refs_2_.refs_4_ = bf16[136,768]{1,0:T(8,128)(2,1)S(1)} collective-permute-done((bf16[136,768]{1,0:T(8,128)(2,1)}, bf16[136,768]{1,0:T(8,128)(2,1)S(1)}, u32[]{:S(2)}, u32[]{:S(2)}) %collective-permute-start.1) | collective-permute-done | bytes 208928 | tf_op jit(solution)/shard_map/ppermute | solution.py:685
  25.9 4.6 %project.1 = (bf16[512,1024]{1,0:T(8,128)(2,1)}, bf16[512,256]{1,0:T(8,128)(2,1)}, bf16[512,512]{1,0:T(8,128)(2,1)}, bf16[128,1024]{1,0:T(8,128)(2,1)}, f32[8,10...) custom-call(s32[3]{0:T(128)} %pad_add_fusion.scalars, bf16[512,1024]{1,0:T(8,128)(2,1)} %bitcast.31, ...), custom_call_target="tpu_custom_call" | custom-call | flops 805306368 | bytes 4855808 | tf_op jit(solution)/shard_map/project/pallas_call | solution.py:58
  34.8 2.5 order_grad.1
  37.3 9.3 %collective-permute-done.8.refs_2_ = bf16[512,512]{1,0:T(8,128)(2,1)S(1)} collective-permute-done((bf16[512,512]{1,0:T(8,128)(2,1)}, bf16[512,512]{1,0:T(8,128)(2,1)S(1)}, u32[]{:S(2)}, u32[]{:S(2)}) %collective-permute-start.8) | collective-permute-done | bytes 524320 | tf_op jit(solution)/shard_map/ppermute | solution.py:688
  51.3 5.3 %attention.1 = (bf16[128,256]{1,0:T(8,128)(2,1)}, bf16[128,256]{1,0:T(8,128)(2,1)}, bf16[128,256]{1,0:T(8,128)(2,1)}, bf16[128,256]{1,0:T(8,128)(2,1)}, f32[4,512]{1,0:T(4,128)}) custom-call(s32[5]{0:T(128)} %pad_add_fusion.1.scalars, s32[1,512]{1,0:T(1,128)} %bitcast.44, bf16[512,256]{1,0:T(8,128)(2,1)} %get-tuple-element.118.q_ref, ...), custom_call_target="tpu_custom_call" | custom-call | flops 1073741824 | bytes 2631680 | tf_op jit(solution)/shard_map/attention/pallas_call | solution.py:58
  58.2 2.6 collective-permute-start.13
  61.1 3.7 %collective-permute-done.13.refs_2_.refs_5_ = bf16[128,256]{1,0:T(8,128)(2,1)S(1)} collective-permute-done((bf16[128,256]{1,0:T(8,128)(2,1)}, bf16[128,256]{1,0:T(8,128)(2,1)S(1)}, u32[]{:S(2)}, u32[]{:S(2)}) %collective-permute-start.13) | collective-permute-done | bytes 65568 | tf_op jit(solution)/shard_map/ppermute | solution.py:691
  64.8 3.5 %collective-permute-done.14.refs_3_.refs_6_ = bf16[128,256]{1,0:T(8,128)(2,1)S(1)} collective-permute-done((bf16[128,256]{1,0:T(8,128)(2,1)}, bf16[128,256]{1,0:T(8,128)(2,1)S(1)}, u32[]{:S(2)}, u32[]{:S(2)}) %collective-permute-start.14) | collective-permute-done | bytes 65568 | tf_op jit(solution)/shard_map/ppermute | solution.py:691
  68.3 6.1 %all-gather.3.cloned.1.call-done = bf16[8192,128]{1,0:T(8,128)(2,1)} async-done(((bf16[256,128]{1,0:T(8,128)(2,1)}), bf16[8192,128]{1,0:T(8,128)(2,1)}) %all-gather.3.cloned.1.call-update) | async-done | bytes 2097168 | tf_op jit(solution)/shard_map/all_gather | solution.py:739
  74.5 3.2 %merge.1 = (f32[128,1024]{1,0:T(8,128)}, bf16[128,1024]{1,0:T(8,128)(2,1)}) custom-call(s32[3]{0:T(128)} %pad_add_fusion.scalars, bf16[128,1024]{1,0:T(8,128)(2,1)} %get-tuple-element.130.rows_ref, f32[8,1024]{1,0:T(8,128)} %get-tuple-element.131.wide_ref, bf16[8,4,256,128]{3,2,1,0:T(8,128)(2,1)} %bitcast.33, ...), custom_call_target="tpu_custom_call" | custom-call | flops 268435456 | bytes 3440640 | tf_op jit(solution)/shard_map/merge/pallas_call | solution.py:58
  82.0 11.8 %collective-permute-done.15.refs_1_.refs_2_ = bf16[128,1024]{1,0:T(8,128)(2,1)S(1)} collective-permute-done((bf16[128,1024]{1,0:T(8,128)(2,1)}, bf16[128,1024]{1,0:T(8,128)(2,1)S(1)}, u32[]{:S(2)}, u32[]{:S(2)}) %collective-permute-start.15) | collective-permute-done | bytes 262176 | tf_op jit(solution)/shard_map/ppermute | solution.py:691
  95.0 2.8 %dense.2 = (bf16[128,1024]{1,0:T(8,128)(2,1)S(1)}, bf16[128,1024]{1,0:T(8,128)(2,1)S(1)}, bf16[128,1024]{1,0:T(8,128)(2,1)S(1)}, bf16[128,1024]{1,0:T(8,128)(2,1...) custom-call(f32[1,1024]{1,0:T(1,128)S(1)} %copy-done.36, ...), custom_call_target="tpu_custom_call" | custom-call | flops 2147483648 | bytes 7348224 | tf_op jit(solution)/shard_map/dense/pallas_call | solution.py:58
  98.6 3.3 %collective-permute-start.22 = (bf16[128,1024]{1,0:T(8,128)(2,1)S(1)}, bf16[128,1024]{1,0:T(8,128)(2,1)S(1)}, u32[]{:S(2)}, u32[]{:S(2)}) collective-permute-start(bf16[128,1024]{1,0:T(8,128)(2,1)S(1)} %get-tuple-element.142), channel_id=1, source_target_pairs={{0,2},{1,3},{2,0},{3,1},{4,6},{5,7},{6,4},{7,5},{8,10},{9,11},{10,... | collective-permute-start | bytes 786440 | tf_op jit(solution)/shard_map/ppermute | solution.py:691
  101.9 2.8 %dense.3 = (bf16[128,1024]{1,0:T(8,128)(2,1)S(1)}, bf16[128,1024]{1,0:T(8,128)(2,1)S(1)}, bf16[128,1024]{1,0:T(8,128)(2,1)S(1)}, bf16[128,1024]{1,0:T(8,128)(2,1...) custom-call(f32[1,1024]{1,0:T(1,128)S(1)} %copy-done.36, ...), custom_call_target="tpu_custom_call" | custom-call | flops 2147483648 | bytes 7348224 | tf_op jit(solution)/shard_map/dense/pallas_call | solution.py:58
  105.2 4.0 %collective-permute-start.25 = (bf16[128,1024]{1,0:T(8,128)(2,1)S(1)}, bf16[128,1024]{1,0:T(8,128)(2,1)S(1)}, u32[]{:S(2)}, u32[]{:S(2)}) collective-permute-start(bf16[128,1024]{1,0:T(8,128)(2,1)S(1)} %get-tuple-element.157), channel_id=1, source_target_pairs={{0,3},{1,2},{2,1},{3,0},{4,7},{5,6},{6,5},{7,4},{8,11},{9,10},{10,... | collective-permute-start | bytes 786440 | tf_op jit(solution)/shard_map/ppermute | solution.py:691
  109.2 3.0 %dense_outer.1.refs_7_ = bf16[8,384,1024]{2,1,0:T(8,128)(2,1)S(1)} custom-call(s32[3]{0:T(128)S(1)} %copy-done.23, bf16[128,1024]{1,0:T(8,128)(2,1)S(1)} %copy-done.22, bf16[128,1024]{1,0:T(8,128)(2,1)S(1)} %collective-permute-done.16.refs_0_.refs_1_, bf16[128,1024]{1,0:T(8,128)(2,1)S(1)} %collective-permute-done.15.refs_1_.refs_2_, ...), custom_call_target="tpu_custom_call" | custom-call | flops 2147483648 | bytes 10485760 | tf_op jit(solution)/shard_map/dense_outer/pallas_call | solution.py:58
  112.2 2.6 copy-done
  116.7 6.1 %collective-permute-done.24.refs_1_ = bf16[128,1024]{1,0:T(8,128)(2,1)S(1)} collective-permute-done((bf16[128,1024]{1,0:T(8,128)(2,1)S(1)}, bf16[128,1024]{1,0:T(8,128)(2,1)S(1)}, u32[]{:S(2)}, u32[]{:S(2)}) %collective-permute-start.24) | collective-permute-done | bytes 262176 | tf_op jit(solution)/shard_map/ppermute | solution.py:691
  123.6 5.5 %hidden_back.1 = (f32[128,1024]{1,0:T(8,128)}, bf16[128,1024]{1,0:T(8,128)(2,1)}, f32[4,1024]{1,0:T(4,128)}, bf16[128,256]{1,0:T(8,128)(2,1)}, bf16[128,256]{1,0...) custom-call(s32[3]{0:T(128)} %pad_add_fusion.scalars, ...), custom_call_target="tpu_custom_call", output_to_operand_aliasing={{7}: (12, {})} | custom-call | flops 268435456 | bytes 5292032 | tf_op jit(solution)/shard_map/hidden_back/pallas_call | solution.py:58
  129.9 2.7 %collective-permute-start.26 = (bf16[128,256]{1,0:T(8,128)(2,1)S(1)}, bf16[128,256]{1,0:T(8,128)(2,1)S(1)}, u32[]{:S(2)}, u32[]{:S(2)}) collective-permute-start(bf16[128,256]{1,0:T(8,128)(2,1)S(1)} %copy-done.59), channel_id=1, source_target_pairs={{0,1},{1,0},{2,3},{3,2},{4,5},{5,4},{6,7},{7,6},{8,9},{9,8},{10,11... | collective-permute-start | bytes 196616 | tf_op jit(solution)/shard_map/ppermute | solution.py:691
  141.3 7.4 %attention_back.1 = (bf16[512,256]{1,0:T(8,128)(2,1)}, bf16[512,512]{1,0:T(8,128)(2,1)}, bf16[512,512]{1,0:T(8,128)(2,1)}, bf16[512,512]{1,0:T(8,128)(2,1)}, bf16[512,512]{1,0:T(8,128)(2,1)}) custom-call(s32[5]{0:T(128)} %pad_add_fusion.1.scalars, s32[1,512]{1,0:T(1,128)} %bitcast.45, f32[4,512]{1,0:T(4,128)} %get-tuple-element.125.lse_ref, ...), custom_call_target="tpu_custom_call" | custom-call | flops 2684354560 | bytes 5253120 | tf_op jit(solution)/shard_map/attention_back/pallas_call | solution.py:58
  148.7 10.1 %collective-permute-done.30.refs_2_ = bf16[128,1024]{1,0:T(8,128)(2,1)S(1)} collective-permute-done((bf16[128,1024]{1,0:T(8,128)(2,1)S(1)}, bf16[128,1024]{1,0:T(8,128)(2,1)S(1)}, u32[]{:S(2)}, u32[]{:S(2)}) %collective-permute-start.30) | collective-permute-done | bytes 262176 | tf_op jit(solution)/shard_map/ppermute | solution.py:691
  163.5 5.8 %collective-permute-start.34 = (bf16[128,1024]{1,0:T(8,128)(2,1)S(1)}, bf16[128,1024]{1,0:T(8,128)(2,1)S(1)}, u32[]{:S(2)}, u32[]{:S(2)}) collective-permute-start(bf16[128,1024]{1,0:T(8,128)(2,1)S(1)} %get-tuple-element.173.refs_0_), channel_id=1, source_target_pairs={{0,2},{1,3},{2,0},{3,1},{4,6},{5,7},{6,4},{7,5},{8,10},{9,11},{10,... | collective-permute-start | bytes 786440 | tf_op jit(solution)/shard_map/ppermute | solution.py:691
  171.3 10.0 %collective-permute-done.34.refs_2_ = bf16[128,1024]{1,0:T(8,128)(2,1)S(1)} collective-permute-done((bf16[128,1024]{1,0:T(8,128)(2,1)S(1)}, bf16[128,1024]{1,0:T(8,128)(2,1)S(1)}, u32[]{:S(2)}, u32[]{:S(2)}) %collective-permute-start.34) | collective-permute-done | bytes 262176 | tf_op jit(solution)/shard_map/ppermute | solution.py:691
  184.3 6.5 %project_back.1 = (bf16[128,1024]{1,0:T(8,128)(2,1)}, bf16[128,1024]{1,0:T(8,128)(2,1)}, bf16[128,1024]{1,0:T(8,128)(2,1)}, bf16[128,1024]{1,0:T(8,128)(2,1)}, b...) custom-call(s32[3]{0:T(128)} %pad_add_fusion.scalars, ...), custom_call_target="tpu_custom_call" | custom-call | flops 1610612736 | bytes 7178240 | tf_op jit(solution)/shard_map/project_back/pallas_call | solution.py:58
  192.5 2.4 collective-permute-start.40
  207.7 8.1 %collective-permute-done.38.refs_1_ = bf16[128,1024]{1,0:T(8,128)(2,1)S(1)} collective-permute-done((bf16[128,1024]{1,0:T(8,128)(2,1)}, bf16[128,1024]{1,0:T(8,128)(2,1)S(1)}, u32[]{:S(2)}, u32[]{:S(2)}) %collective-permute-start.38) | collective-permute-done | bytes 262176 | tf_op jit(solution)/shard_map/ppermute | solution.py:691
  219.8 2.7 %collective-permute-start.43 = (bf16[160,1024]{1,0:T(8,128)(2,1)S(1)}, bf16[160,1024]{1,0:T(8,128)(2,1)S(1)}, u32[]{:S(2)}, u32[]{:S(2)}) collective-permute-start(bf16[160,1024]{1,0:T(8,128)(2,1)S(1)} %get-tuple-element.195), channel_id=1, source_target_pairs={{0,3},{1,2},{2,1},{3,0},{4,7},{5,6},{6,5},{7,4},{8,11},{9,10},{10,... | collective-permute-start | bytes 983048 | tf_op jit(solution)/shard_map/ppermute | solution.py:691
  225.9 3.9 %all-to-all-start = ((f32[32,8,128]{2,1,0:T(8,128)}), f32[32,8,128]{2,1,0:T(8,128)S(1)}, u32[]{:S(2)}, u32[]{:S(2)}) async-start(f32[32,8,128]{2,1,0:T(8,128)} %small.1), calls=%async_computation.2 | async-start | bytes 262144 | tf_op jit(solution)/shard_map/all_to_all | solution.py:1006
  229.8 12.8 %reduce-scatter.5.cloned.1.call-done.in_ref = bf16[128,768]{1,0:T(8,128)(2,1)} async-done(((bf16[1024,768]{1,0:T(8,128)(2,1)}), bf16[128,768]{1,0:T(8,128)(2,1)}) %reduce-scatter.5.cloned.1.call-update) | async-done | bytes 196624 | tf_op jit(solution)/shard_map/reduce_scatter | solution.py:956
  244.3 6.4 %collective-permute-done.42.refs_2_ = bf16[160,1024]{1,0:T(8,128)(2,1)S(1)} collective-permute-done((bf16[160,1024]{1,0:T(8,128)(2,1)S(1)}, bf16[160,1024]{1,0:T(8,128)(2,1)S(1)}, u32[]{:S(2)}, u32[]{:S(2)}) %collective-permute-start.42) | collective-permute-done | bytes 327712 | tf_op jit(solution)/shard_map/ppermute | solution.py:691
  (219 shorter events, 78.2 us)
Async XLA Ops:
  7.2 67.3 %all-gather.3.cloned.1.call-start = ((), (), s32[]{:S(2)}) async-start(), calls=%async_computation.5 | async-start | bytes 2162688 | tf_op jit(solution)/shard_map/all_gather | solution.py:739
  7.9 196.6 %reduce-scatter.3.cloned.1.call-start = ((), (), s32[]{:S(2)}) async-start(), calls=%async_computation.3 | async-start | bytes 7077888 | tf_op jit(solution)/shard_map/reduce_scatter | solution.py:956
  9.7 10.1 %collective-permute-start.2 = (bf16[136,768]{1,0:T(8,128)(2,1)}, bf16[136,768]{1,0:T(8,128)(2,1)S(1)}, u32[]{:S(2)}, u32[]{:S(2)}) collective-permute-start(bf16[136,768]{1,0:T(8,128)(2,1)} %pack.1.refs_0_.refs_2_), channel_id=1, source_target_pairs={{0,24},{4,28},{8,16},{12,20},{16,8},{20,12},{24,0},{28,4},{1,25},{... | collective-permute-start | bytes 626696 | tf_op jit(solution)/shard_map/ppermute | solution.py:685
  30.5 16.2 %collective-permute-start.8 = (bf16[512,512]{1,0:T(8,128)(2,1)}, bf16[512,512]{1,0:T(8,128)(2,1)S(1)}, u32[]{:S(2)}, u32[]{:S(2)}) collective-permute-start(bf16[512,512]{1,0:T(8,128)(2,1)} %get-tuple-element.119.refs_0_), channel_id=1, source_target_pairs={{0,8},{4,12},{8,0},{12,4},{1,9},{5,13},{9,1},{13,5},{2,10},{6,14},... | collective-permute-start | bytes 1572872 | tf_op jit(solution)/shard_map/ppermute | solution.py:688
  34.2 14.7 %collective-permute-start.11 = (bf16[256,1024]{1,0:T(8,128)(2,1)}, bf16[256,1024]{1,0:T(8,128)(2,1)S(1)}, u32[]{:S(2)}, u32[]{:S(2)}) collective-permute-start(bf16[256,1024]{1,0:T(8,128)(2,1)} %turn.1.refs_4_), channel_id=1, source_target_pairs={{0,4},{4,0},{8,12},{12,8},{1,5},{5,1},{9,13},{13,9},{2,6},{6,2},{1... | collective-permute-start | bytes 1572872 | tf_op jit(solution)/shard_map/ppermute | solution.py:688
  34.2 16.1 %collective-permute-start.10 = (bf16[256,1024]{1,0:T(8,128)(2,1)}, bf16[256,1024]{1,0:T(8,128)(2,1)S(1)}, u32[]{:S(2)}, u32[]{:S(2)}) collective-permute-start(bf16[256,1024]{1,0:T(8,128)(2,1)} %turn.1.refs_4_), channel_id=1, source_target_pairs={{0,16},{4,20},{8,24},{12,28},{16,0},{20,4},{24,8},{28,12},{1,17},{... | collective-permute-start | bytes 1572872 | tf_op jit(solution)/shard_map/ppermute | solution.py:685
  47.2 30.4 %collective-permute-start.18 = (bf16[256,1024]{1,0:T(8,128)(2,1)}, bf16[256,1024]{1,0:T(8,128)(2,1)S(1)}, u32[]{:S(2)}, u32[]{:S(2)}) collective-permute-start(bf16[256,1024]{1,0:T(8,128)(2,1)} %turn.1.refs_4_), channel_id=1, source_target_pairs={{0,24},{4,28},{8,16},{12,20},{16,8},{20,12},{24,0},{28,4},{1,25},{... | collective-permute-start | bytes 1572872 | tf_op jit(solution)/shard_map/ppermute | solution.py:685
  48.9 28.7 %collective-permute-start.17 = (bf16[256,1024]{1,0:T(8,128)(2,1)}, bf16[256,1024]{1,0:T(8,128)(2,1)S(1)}, u32[]{:S(2)}, u32[]{:S(2)}) collective-permute-start(bf16[256,1024]{1,0:T(8,128)(2,1)} %turn.1.refs_4_), channel_id=1, source_target_pairs={{0,8},{4,12},{8,0},{12,4},{16,24},{20,28},{24,16},{28,20},{1,9},{5... | collective-permute-start | bytes 1572872 | tf_op jit(solution)/shard_map/ppermute | solution.py:685
  77.6 16.4 %collective-permute-start.19 = (bf16[256,1024]{1,0:T(8,128)(2,1)S(1)}, bf16[256,1024]{1,0:T(8,128)(2,1)S(1)}, u32[]{:S(2)}, u32[]{:S(2)}) collective-permute-start(bf16[256,1024]{1,0:T(8,128)(2,1)S(1)} %collective-permute-done.17.refs_5_), channel_id=1, source_target_pairs={{0,4},{4,0},{8,12},{12,8},{1,5},{5,1},{9,13},{13,9},{2,6},{6,2},{1... | collective-permute-start | bytes 1572872 | tf_op jit(solution)/shard_map/ppermute | solution.py:688
  78.0 16.1 %collective-permute-start.20 = (bf16[256,1024]{1,0:T(8,128)(2,1)S(1)}, bf16[256,1024]{1,0:T(8,128)(2,1)S(1)}, u32[]{:S(2)}, u32[]{:S(2)}) collective-permute-start(bf16[256,1024]{1,0:T(8,128)(2,1)S(1)} %collective-permute-done.10.refs_6_), channel_id=1, source_target_pairs={{0,4},{4,0},{8,12},{12,8},{1,5},{5,1},{9,13},{13,9},{2,6},{6,2},{1... | collective-permute-start | bytes 1572872 | tf_op jit(solution)/shard_map/ppermute | solution.py:688
  78.2 15.8 %collective-permute-start.21 = (bf16[256,1024]{1,0:T(8,128)(2,1)S(1)}, bf16[256,1024]{1,0:T(8,128)(2,1)S(1)}, u32[]{:S(2)}, u32[]{:S(2)}) collective-permute-start(bf16[256,1024]{1,0:T(8,128)(2,1)S(1)} %collective-permute-done.18.refs_7_), channel_id=1, source_target_pairs={{0,4},{4,0},{8,12},{12,8},{1,5},{5,1},{9,13},{13,9},{2,6},{6,2},{1... | collective-permute-start | bytes 1572872 | tf_op jit(solution)/shard_map/ppermute | solution.py:688
  78.5 15.3 %collective-permute-start.15 = (bf16[128,1024]{1,0:T(8,128)(2,1)}, bf16[128,1024]{1,0:T(8,128)(2,1)S(1)}, u32[]{:S(2)}, u32[]{:S(2)}) collective-permute-start(bf16[128,1024]{1,0:T(8,128)(2,1)} %get-tuple-element.134.refs_0_), channel_id=1, source_target_pairs={{0,2},{1,3},{2,0},{3,1},{4,6},{5,7},{6,4},{7,5},{8,10},{9,11},{10,... | collective-permute-start | bytes 786440 | tf_op jit(solution)/shard_map/ppermute | solution.py:691
  80.4 13.6 %collective-permute-start.16 = (bf16[128,1024]{1,0:T(8,128)(2,1)}, bf16[128,1024]{1,0:T(8,128)(2,1)S(1)}, u32[]{:S(2)}, u32[]{:S(2)}) collective-permute-start(bf16[128,1024]{1,0:T(8,128)(2,1)} %get-tuple-element.134.refs_0_), channel_id=1, source_target_pairs={{0,1},{1,0},{2,3},{3,2},{4,5},{5,4},{6,7},{7,6},{8,9},{9,8},{10,11... | collective-permute-start | bytes 786440 | tf_op jit(solution)/shard_map/ppermute | solution.py:691
  98.6 17.3 %collective-permute-start.22 = (bf16[128,1024]{1,0:T(8,128)(2,1)S(1)}, bf16[128,1024]{1,0:T(8,128)(2,1)S(1)}, u32[]{:S(2)}, u32[]{:S(2)}) collective-permute-start(bf16[128,1024]{1,0:T(8,128)(2,1)S(1)} %get-tuple-element.142), channel_id=1, source_target_pairs={{0,2},{1,3},{2,0},{3,1},{4,6},{5,7},{6,4},{7,5},{8,10},{9,11},{10,... | collective-permute-start | bytes 786440 | tf_op jit(solution)/shard_map/ppermute | solution.py:691
  104.7 18.1 %collective-permute-start.24 = (bf16[128,1024]{1,0:T(8,128)(2,1)S(1)}, bf16[128,1024]{1,0:T(8,128)(2,1)S(1)}, u32[]{:S(2)}, u32[]{:S(2)}) collective-permute-start(bf16[128,1024]{1,0:T(8,128)(2,1)S(1)} %get-tuple-element.156), channel_id=1, source_target_pairs={{0,1},{1,0},{2,3},{3,2},{4,5},{5,4},{6,7},{7,6},{8,9},{9,8},{10,11... | collective-permute-start | bytes 786440 | tf_op jit(solution)/shard_map/ppermute | solution.py:691
  105.2 17.6 %collective-permute-start.25 = (bf16[128,1024]{1,0:T(8,128)(2,1)S(1)}, bf16[128,1024]{1,0:T(8,128)(2,1)S(1)}, u32[]{:S(2)}, u32[]{:S(2)}) collective-permute-start(bf16[128,1024]{1,0:T(8,128)(2,1)S(1)} %get-tuple-element.157), channel_id=1, source_target_pairs={{0,3},{1,2},{2,1},{3,0},{4,7},{5,6},{6,5},{7,4},{8,11},{9,10},{10,... | collective-permute-start | bytes 786440 | tf_op jit(solution)/shard_map/ppermute | solution.py:691
  129.2 113.4 %reduce-scatter.5.cloned.1.call-start = ((), (), s32[]{:S(2)}) async-start(), calls=%async_computation.4 | async-start | bytes 1769472 | tf_op jit(solution)/shard_map/reduce_scatter | solution.py:956
  135.1 13.7 %collective-permute-start.29 = (bf16[128,1024]{1,0:T(8,128)(2,1)S(1)}, bf16[128,1024]{1,0:T(8,128)(2,1)S(1)}, u32[]{:S(2)}, u32[]{:S(2)}) collective-permute-start(bf16[128,1024]{1,0:T(8,128)(2,1)S(1)} %copy-done.35), channel_id=1, source_target_pairs={{0,1},{1,0},{2,3},{3,2},{4,5},{5,4},{6,7},{7,6},{8,9},{9,8},{10,11... | collective-permute-start | bytes 786440 | tf_op jit(solution)/shard_map/ppermute | solution.py:691
  136.1 22.8 %collective-permute-start.30 = (bf16[128,1024]{1,0:T(8,128)(2,1)S(1)}, bf16[128,1024]{1,0:T(8,128)(2,1)S(1)}, u32[]{:S(2)}, u32[]{:S(2)}) collective-permute-start(bf16[128,1024]{1,0:T(8,128)(2,1)S(1)} %copy-done.31), channel_id=1, source_target_pairs={{0,2},{1,3},{2,0},{3,1},{4,6},{5,7},{6,4},{7,5},{8,10},{9,11},{10,... | collective-permute-start | bytes 786440 | tf_op jit(solution)/shard_map/ppermute | solution.py:691
  138.0 20.9 %collective-permute-start.31 = (bf16[128,1024]{1,0:T(8,128)(2,1)S(1)}, bf16[128,1024]{1,0:T(8,128)(2,1)S(1)}, u32[]{:S(2)}, u32[]{:S(2)}) collective-permute-start(bf16[128,1024]{1,0:T(8,128)(2,1)S(1)} %copy-done.33), channel_id=1, source_target_pairs={{0,3},{1,2},{2,1},{3,0},{4,7},{5,6},{6,5},{7,4},{8,11},{9,10},{10,... | collective-permute-start | bytes 786440 | tf_op jit(solution)/shard_map/ppermute | solution.py:691
  158.9 10.5 %collective-permute-start.36 = (bf16[512,512]{1,0:T(8,128)(2,1)}, bf16[512,512]{1,0:T(8,128)(2,1)S(1)}, u32[]{:S(2)}, u32[]{:S(2)}) collective-permute-start(bf16[512,512]{1,0:T(8,128)(2,1)} %get-tuple-element.176), channel_id=1, source_target_pairs={{0,4},{4,0},{8,12},{12,8},{1,5},{5,1},{9,13},{13,9},{2,6},{6,2},{1... | collective-permute-start | bytes 1572872 | tf_op jit(solution)/shard_map/ppermute | solution.py:688
  163.0 20.5 %collective-permute-start.37 = (bf16[512,512]{1,0:T(8,128)(2,1)S(1)}, bf16[512,512]{1,0:T(8,128)(2,1)S(1)}, u32[]{:S(2)}, u32[]{:S(2)}) collective-permute-start(bf16[512,512]{1,0:T(8,128)(2,1)S(1)} %get-tuple-element.177), channel_id=1, source_target_pairs={{0,8},{4,12},{8,0},{12,4},{1,9},{5,13},{9,1},{13,5},{2,10},{6,14},... | collective-permute-start | bytes 1572872 | tf_op jit(solution)/shard_map/ppermute | solution.py:688
  163.5 17.8 %collective-permute-start.34 = (bf16[128,1024]{1,0:T(8,128)(2,1)S(1)}, bf16[128,1024]{1,0:T(8,128)(2,1)S(1)}, u32[]{:S(2)}, u32[]{:S(2)}) collective-permute-start(bf16[128,1024]{1,0:T(8,128)(2,1)S(1)} %get-tuple-element.173.refs_0_), channel_id=1, source_target_pairs={{0,2},{1,3},{2,0},{3,1},{4,6},{5,7},{6,4},{7,5},{8,10},{9,11},{10,... | collective-permute-start | bytes 786440 | tf_op jit(solution)/shard_map/ppermute | solution.py:691
  169.4 12.0 %collective-permute-start.33 = (bf16[128,1024]{1,0:T(8,128)(2,1)S(1)}, bf16[128,1024]{1,0:T(8,128)(2,1)S(1)}, u32[]{:S(2)}, u32[]{:S(2)}) collective-permute-start(bf16[128,1024]{1,0:T(8,128)(2,1)S(1)} %get-tuple-element.173.refs_0_), channel_id=1, source_target_pairs={{0,1},{1,0},{2,3},{3,2},{4,5},{5,4},{6,7},{7,6},{8,9},{9,8},{10,11... | collective-permute-start | bytes 786440 | tf_op jit(solution)/shard_map/ppermute | solution.py:691
  190.9 12.1 %collective-permute-start.35 = (bf16[128,1024]{1,0:T(8,128)(2,1)S(1)}, bf16[128,1024]{1,0:T(8,128)(2,1)S(1)}, u32[]{:S(2)}, u32[]{:S(2)}) collective-permute-start(bf16[128,1024]{1,0:T(8,128)(2,1)S(1)} %collective-permute-done.34.refs_2_), channel_id=1, source_target_pairs={{0,1},{1,0},{2,3},{3,2},{4,5},{5,4},{6,7},{7,6},{8,9},{9,8},{10,11... | collective-permute-start | bytes 786440 | tf_op jit(solution)/shard_map/ppermute | solution.py:691
  192.5 15.2 %collective-permute-start.40 = (bf16[128,1024]{1,0:T(8,128)(2,1)}, bf16[128,1024]{1,0:T(8,128)(2,1)S(1)}, u32[]{:S(2)}, u32[]{:S(2)}) collective-permute-start(bf16[128,1024]{1,0:T(8,128)(2,1)} %get-tuple-element.184.refs_3_), channel_id=1, source_target_pairs={{0,3},{1,2},{2,1},{3,0},{4,7},{5,6},{6,5},{7,4},{8,11},{9,10},{10,... | collective-permute-start | bytes 786440 | tf_op jit(solution)/shard_map/ppermute | solution.py:691
  194.8 20.9 %collective-permute-start.38 = (bf16[128,1024]{1,0:T(8,128)(2,1)}, bf16[128,1024]{1,0:T(8,128)(2,1)S(1)}, u32[]{:S(2)}, u32[]{:S(2)}) collective-permute-start(bf16[128,1024]{1,0:T(8,128)(2,1)} %get-tuple-element.182.refs_1_), channel_id=1, source_target_pairs={{0,1},{1,0},{2,3},{3,2},{4,5},{5,4},{6,7},{7,6},{8,9},{9,8},{10,11... | collective-permute-start | bytes 786440 | tf_op jit(solution)/shard_map/ppermute | solution.py:691
  195.4 22.6 %collective-permute-start.39 = (bf16[128,1024]{1,0:T(8,128)(2,1)}, bf16[128,1024]{1,0:T(8,128)(2,1)}, u32[]{:S(2)}, u32[]{:S(2)}) collective-permute-start(bf16[128,1024]{1,0:T(8,128)(2,1)} %get-tuple-element.183.refs_2_), channel_id=1, source_target_pairs={{0,2},{1,3},{2,0},{3,1},{4,6},{5,7},{6,4},{7,5},{8,10},{9,11},{10,... | collective-permute-start | bytes 786440 | tf_op jit(solution)/shard_map/ppermute | solution.py:691
  219.8 24.5 %collective-permute-start.43 = (bf16[160,1024]{1,0:T(8,128)(2,1)S(1)}, bf16[160,1024]{1,0:T(8,128)(2,1)S(1)}, u32[]{:S(2)}, u32[]{:S(2)}) collective-permute-start(bf16[160,1024]{1,0:T(8,128)(2,1)S(1)} %get-tuple-element.195), channel_id=1, source_target_pairs={{0,3},{1,2},{2,1},{3,0},{4,7},{5,6},{6,5},{7,4},{8,11},{9,10},{10,... | collective-permute-start | bytes 983048 | tf_op jit(solution)/shard_map/ppermute | solution.py:691
  222.5 21.8 %collective-permute-start.41 = (bf16[160,1024]{1,0:T(8,128)(2,1)S(1)}, bf16[160,1024]{1,0:T(8,128)(2,1)S(1)}, u32[]{:S(2)}, u32[]{:S(2)}) collective-permute-start(bf16[160,1024]{1,0:T(8,128)(2,1)S(1)} %get-tuple-element.193), channel_id=1, source_target_pairs={{0,1},{1,0},{2,3},{3,2},{4,5},{5,4},{6,7},{7,6},{8,9},{9,8},{10,11... | collective-permute-start | bytes 983048 | tf_op jit(solution)/shard_map/ppermute | solution.py:691
  222.5 28.1 %collective-permute-start.42 = (bf16[160,1024]{1,0:T(8,128)(2,1)S(1)}, bf16[160,1024]{1,0:T(8,128)(2,1)S(1)}, u32[]{:S(2)}, u32[]{:S(2)}) collective-permute-start(bf16[160,1024]{1,0:T(8,128)(2,1)S(1)} %get-tuple-element.194), channel_id=1, source_target_pairs={{0,2},{1,3},{2,0},{3,1},{4,6},{5,7},{6,4},{7,5},{8,10},{9,11},{10,... | collective-permute-start | bytes 983048 | tf_op jit(solution)/shard_map/ppermute | solution.py:691
  225.9 26.6 %all-to-all-start = ((f32[32,8,128]{2,1,0:T(8,128)}), f32[32,8,128]{2,1,0:T(8,128)S(1)}, u32[]{:S(2)}, u32[]{:S(2)}) async-start(f32[32,8,128]{2,1,0:T(8,128)} %small.1), calls=%async_computation.2 | async-start | bytes 262144 | tf_op jit(solution)/shard_map/all_to_all | solution.py:1006
  (77 other events, 810.8 us)
Sparse Core Ops, SparseCore 0:
  10.9 63.4 all-gather.2
  129.3 70.9 reduce-scatter.2
  204.0 38.5 reduce-scatter.4

commit v2 on v1

--- a/solution.py
+++ b/solution.py
@@ -19,6 +19,8 @@
     "dense_total",
     "input_back",
     "place",
+    "small_total",
+    "attend_total",
 )
 F32 = jnp.float32
 BF16 = jnp.bfloat16

time: 262 us -> 261 us (level)
  transfers between devices with their start and end apart: 48 -> 48, of which waited for: 23 -> 23; matrix products, arithmetic and copies ran while one was open for 2% -> 2% of each run, Pallas kernels for 21% -> 20%
where the time goes in v2:
time: 261 us
  waiting for transfers between devices  105 us (40%)
  Pallas kernels  59.8 us (23%)
  starting transfers between devices  59.3 us (23%)
  local copies, waits for them, and re-layouts  20.6 us (8%)
  between operations  14.2 us (5%)
    ppermute x24, waiting for transfers between devices, tp_swap(): return lax.ppermute(value, 'tp', [(i, i ^ offset) for i in range(n_tp)])  65.2 us
    pallas_call x23, Pallas kernels, call(): pl.pallas_call(kernel, grid=(1,), out_shape=tuple(outs), in_specs=[pl.Blo...  59.8 us
    ppermute x24, starting transfers between devices, tp_swap(): return lax.ppermute(value, 'tp', [(i, i ^ offset) for i in range(n_tp)])  41.3 us
    unnamed x122, local copies, waits for them, and re-layouts  19 us
    ppermute x14, waiting for transfers between devices, ctx_swap(): return lax.ppermute(value, 'ctx', [(i, i ^ offset) for i in range(n_ctx)])  13.7 us
    reduce_scatter x2, waiting for transfers between devices, scattered(): return lax.psum_scatter(flat, plane, scatter_dimension=0, tiled=True)  12.7 us
    ppermute x6, starting transfers between devices, plane_swap(): return lax.ppermute(value, plane, [(i, i ^ offset) for i in range(group)])  8.25 us
    ppermute x6, waiting for transfers between devices, plane_swap(): return lax.ppermute(value, plane, [(i, i ^ offset) for i in range(group)])  6.12 us
  transfers between devices with their start and end apart: 48, of which 23 were waited for; matrix products, arithmetic and copies ran while one was open for 2% of the time, Pallas kernels for 20%

profile of v2, /device:TPU:0, one launch (start us, length us, event | category | flops | bytes accessed | tf_op | source)
XLA Modules:
  0.0 260.9 jit_solution(14174633217580084099)
XLA Ops:
  9.7 3.9 %collective-permute-start.2 = (bf16[136,768]{1,0:T(8,128)(2,1)}, bf16[136,768]{1,0:T(8,128)(2,1)S(1)}, u32[]{:S(2)}, u32[]{:S(2)}) collective-permute-start(bf16[136,768]{1,0:T(8,128)(2,1)} %pack.1.refs_0_.refs_2_), channel_id=1, source_target_pairs={{0,24},{4,28},{8,16},{12,20},{16,8},{20,12},{24,0},{28,4},{1,25},{... | collective-permute-start | bytes 626696 | tf_op jit(solution)/shard_map/ppermute | solution.py:687
  19.9 3.6 %collective-permute-done.1.refs_2_.refs_4_ = bf16[136,768]{1,0:T(8,128)(2,1)S(1)} collective-permute-done((bf16[136,768]{1,0:T(8,128)(2,1)}, bf16[136,768]{1,0:T(8,128)(2,1)S(1)}, u32[]{:S(2)}, u32[]{:S(2)}) %collective-permute-start.1) | collective-permute-done | bytes 208928 | tf_op jit(solution)/shard_map/ppermute | solution.py:687
  25.9 4.6 %project.1 = (bf16[512,1024]{1,0:T(8,128)(2,1)}, bf16[512,256]{1,0:T(8,128)(2,1)}, bf16[512,512]{1,0:T(8,128)(2,1)}, bf16[128,1024]{1,0:T(8,128)(2,1)}, f32[8,10...) custom-call(s32[3]{0:T(128)} %pad_add_fusion.scalars, bf16[512,1024]{1,0:T(8,128)(2,1)} %bitcast.31, ...), custom_call_target="tpu_custom_call" | custom-call | flops 805306368 | bytes 4855808 | tf_op jit(solution)/shard_map/project/pallas_call | solution.py:60
  34.8 2.5 order_grad.1
  37.3 9.3 %collective-permute-done.8.refs_2_ = bf16[512,512]{1,0:T(8,128)(2,1)S(1)} collective-permute-done((bf16[512,512]{1,0:T(8,128)(2,1)}, bf16[512,512]{1,0:T(8,128)(2,1)S(1)}, u32[]{:S(2)}, u32[]{:S(2)}) %collective-permute-start.8) | collective-permute-done | bytes 524320 | tf_op jit(solution)/shard_map/ppermute | solution.py:690
  51.3 5.3 %attention.1 = (bf16[128,256]{1,0:T(8,128)(2,1)}, bf16[128,256]{1,0:T(8,128)(2,1)}, bf16[128,256]{1,0:T(8,128)(2,1)}, bf16[128,256]{1,0:T(8,128)(2,1)}, f32[4,512]{1,0:T(4,128)}) custom-call(s32[5]{0:T(128)} %pad_add_fusion.1.scalars, s32[1,512]{1,0:T(1,128)} %bitcast.44, bf16[512,256]{1,0:T(8,128)(2,1)} %get-tuple-element.118.q_ref, ...), custom_call_target="tpu_custom_call" | custom-call | flops 1073741824 | bytes 2631680 | tf_op jit(solution)/shard_map/attention/pallas_call | solution.py:60
  58.2 2.6 collective-permute-start.13
  61.1 3.7 %collective-permute-done.13.refs_2_.refs_5_ = bf16[128,256]{1,0:T(8,128)(2,1)S(1)} collective-permute-done((bf16[128,256]{1,0:T(8,128)(2,1)}, bf16[128,256]{1,0:T(8,128)(2,1)S(1)}, u32[]{:S(2)}, u32[]{:S(2)}) %collective-permute-start.13) | collective-permute-done | bytes 65568 | tf_op jit(solution)/shard_map/ppermute | solution.py:693
  64.8 3.5 %collective-permute-done.14.refs_3_.refs_6_ = bf16[128,256]{1,0:T(8,128)(2,1)S(1)} collective-permute-done((bf16[128,256]{1,0:T(8,128)(2,1)}, bf16[128,256]{1,0:T(8,128)(2,1)S(1)}, u32[]{:S(2)}, u32[]{:S(2)}) %collective-permute-start.14) | collective-permute-done | bytes 65568 | tf_op jit(solution)/shard_map/ppermute | solution.py:693
  68.3 6.1 %all-gather.3.cloned.1.call-done = bf16[8192,128]{1,0:T(8,128)(2,1)} async-done(((bf16[256,128]{1,0:T(8,128)(2,1)}), bf16[8192,128]{1,0:T(8,128)(2,1)}) %all-gather.3.cloned.1.call-update) | async-done | bytes 2097168 | tf_op jit(solution)/shard_map/all_gather | solution.py:741
  74.5 3.2 %merge.1 = (f32[128,1024]{1,0:T(8,128)}, bf16[128,1024]{1,0:T(8,128)(2,1)}) custom-call(s32[3]{0:T(128)} %pad_add_fusion.scalars, bf16[128,1024]{1,0:T(8,128)(2,1)} %get-tuple-element.130.rows_ref, f32[8,1024]{1,0:T(8,128)} %get-tuple-element.131.wide_ref, bf16[8,4,256,128]{3,2,1,0:T(8,128)(2,1)} %bitcast.33, ...), custom_call_target="tpu_custom_call" | custom-call | flops 268435456 | bytes 3440640 | tf_op jit(solution)/shard_map/merge/pallas_call | solution.py:60
  82.0 11.8 %collective-permute-done.15.refs_1_.refs_2_ = bf16[128,1024]{1,0:T(8,128)(2,1)S(1)} collective-permute-done((bf16[128,1024]{1,0:T(8,128)(2,1)}, bf16[128,1024]{1,0:T(8,128)(2,1)S(1)}, u32[]{:S(2)}, u32[]{:S(2)}) %collective-permute-start.15) | collective-permute-done | bytes 262176 | tf_op jit(solution)/shard_map/ppermute | solution.py:693
  95.0 2.8 %dense.2 = (bf16[128,1024]{1,0:T(8,128)(2,1)S(1)}, bf16[128,1024]{1,0:T(8,128)(2,1)S(1)}, bf16[128,1024]{1,0:T(8,128)(2,1)S(1)}, bf16[128,1024]{1,0:T(8,128)(2,1...) custom-call(f32[1,1024]{1,0:T(1,128)S(1)} %copy-done.37, ...), custom_call_target="tpu_custom_call" | custom-call | flops 2147483648 | bytes 7348224 | tf_op jit(solution)/shard_map/dense/pallas_call | solution.py:60
  98.6 3.3 %collective-permute-start.22 = (bf16[128,1024]{1,0:T(8,128)(2,1)S(1)}, bf16[128,1024]{1,0:T(8,128)(2,1)S(1)}, u32[]{:S(2)}, u32[]{:S(2)}) collective-permute-start(bf16[128,1024]{1,0:T(8,128)(2,1)S(1)} %get-tuple-element.142), channel_id=1, source_target_pairs={{0,2},{1,3},{2,0},{3,1},{4,6},{5,7},{6,4},{7,5},{8,10},{9,11},{10,... | collective-permute-start | bytes 786440 | tf_op jit(solution)/shard_map/ppermute | solution.py:693
  101.9 2.8 %dense.3 = (bf16[128,1024]{1,0:T(8,128)(2,1)S(1)}, bf16[128,1024]{1,0:T(8,128)(2,1)S(1)}, bf16[128,1024]{1,0:T(8,128)(2,1)S(1)}, bf16[128,1024]{1,0:T(8,128)(2,1...) custom-call(f32[1,1024]{1,0:T(1,128)S(1)} %copy-done.37, ...), custom_call_target="tpu_custom_call" | custom-call | flops 2147483648 | bytes 7348224 | tf_op jit(solution)/shard_map/dense/pallas_call | solution.py:60
  105.2 4.0 %collective-permute-start.25 = (bf16[128,1024]{1,0:T(8,128)(2,1)S(1)}, bf16[128,1024]{1,0:T(8,128)(2,1)S(1)}, u32[]{:S(2)}, u32[]{:S(2)}) collective-permute-start(bf16[128,1024]{1,0:T(8,128)(2,1)S(1)} %get-tuple-element.157), channel_id=1, source_target_pairs={{0,3},{1,2},{2,1},{3,0},{4,7},{5,6},{6,5},{7,4},{8,11},{9,10},{10,... | collective-permute-start | bytes 786440 | tf_op jit(solution)/shard_map/ppermute | solution.py:693
  109.2 3.0 %dense_outer.1.refs_7_ = bf16[8,384,1024]{2,1,0:T(8,128)(2,1)S(1)} custom-call(s32[3]{0:T(128)S(1)} %copy-done.24, bf16[128,1024]{1,0:T(8,128)(2,1)S(1)} %copy-done.22, bf16[128,1024]{1,0:T(8,128)(2,1)S(1)} %collective-permute-done.16.refs_0_.refs_1_, bf16[128,1024]{1,0:T(8,128)(2,1)S(1)} %collective-permute-done.15.refs_1_.refs_2_, ...), custom_call_target="tpu_custom_call" | custom-call | flops 2147483648 | bytes 10485760 | tf_op jit(solution)/shard_map/dense_outer/pallas_call | solution.py:60
  112.2 2.6 copy-done
  116.7 6.1 %collective-permute-done.24.refs_1_ = bf16[128,1024]{1,0:T(8,128)(2,1)S(1)} collective-permute-done((bf16[128,1024]{1,0:T(8,128)(2,1)S(1)}, bf16[128,1024]{1,0:T(8,128)(2,1)S(1)}, u32[]{:S(2)}, u32[]{:S(2)}) %collective-permute-start.24) | collective-permute-done | bytes 262176 | tf_op jit(solution)/shard_map/ppermute | solution.py:693
  123.6 5.5 %hidden_back.1 = (f32[128,1024]{1,0:T(8,128)}, bf16[128,1024]{1,0:T(8,128)(2,1)}, f32[4,1024]{1,0:T(4,128)}, bf16[128,256]{1,0:T(8,128)(2,1)}, bf16[128,256]{1,0...) custom-call(s32[3]{0:T(128)} %pad_add_fusion.scalars, ...), custom_call_target="tpu_custom_call", output_to_operand_aliasing={{7}: (12, {})} | custom-call | flops 268435456 | bytes 5292032 | tf_op jit(solution)/shard_map/hidden_back/pallas_call | solution.py:60
  129.9 2.7 %collective-permute-start.26 = (bf16[128,256]{1,0:T(8,128)(2,1)S(1)}, bf16[128,256]{1,0:T(8,128)(2,1)S(1)}, u32[]{:S(2)}, u32[]{:S(2)}) collective-permute-start(bf16[128,256]{1,0:T(8,128)(2,1)S(1)} %copy-done.59), channel_id=1, source_target_pairs={{0,1},{1,0},{2,3},{3,2},{4,5},{5,4},{6,7},{7,6},{8,9},{9,8},{10,11... | collective-permute-start | bytes 196616 | tf_op jit(solution)/shard_map/ppermute | solution.py:693
  141.3 7.4 %attention_back.1 = (bf16[512,256]{1,0:T(8,128)(2,1)}, bf16[512,512]{1,0:T(8,128)(2,1)}, bf16[512,512]{1,0:T(8,128)(2,1)}, bf16[512,512]{1,0:T(8,128)(2,1)}, bf16[512,512]{1,0:T(8,128)(2,1)}) custom-call(s32[5]{0:T(128)} %pad_add_fusion.1.scalars, s32[1,512]{1,0:T(1,128)} %bitcast.45, f32[4,512]{1,0:T(4,128)} %get-tuple-element.125.lse_ref, ...), custom_call_target="tpu_custom_call" | custom-call | flops 2684354560 | bytes 5253120 | tf_op jit(solution)/shard_map/attention_back/pallas_call | solution.py:60
  148.7 10.1 %collective-permute-done.30.refs_2_ = bf16[128,1024]{1,0:T(8,128)(2,1)S(1)} collective-permute-done((bf16[128,1024]{1,0:T(8,128)(2,1)S(1)}, bf16[128,1024]{1,0:T(8,128)(2,1)S(1)}, u32[]{:S(2)}, u32[]{:S(2)}) %collective-permute-start.30) | collective-permute-done | bytes 262176 | tf_op jit(solution)/shard_map/ppermute | solution.py:693
  164.8 5.4 %collective-permute-start.34 = (bf16[128,1024]{1,0:T(8,128)(2,1)S(1)}, bf16[128,1024]{1,0:T(8,128)(2,1)S(1)}, u32[]{:S(2)}, u32[]{:S(2)}) collective-permute-start(bf16[128,1024]{1,0:T(8,128)(2,1)S(1)} %get-tuple-element.173.refs_0_), channel_id=1, source_target_pairs={{0,2},{1,3},{2,0},{3,1},{4,6},{5,7},{6,4},{7,5},{8,10},{9,11},{10,... | collective-permute-start | bytes 786440 | tf_op jit(solution)/shard_map/ppermute | solution.py:693
  172.1 10.0 %collective-permute-done.34.refs_2_ = bf16[128,1024]{1,0:T(8,128)(2,1)S(1)} collective-permute-done((bf16[128,1024]{1,0:T(8,128)(2,1)S(1)}, bf16[128,1024]{1,0:T(8,128)(2,1)S(1)}, u32[]{:S(2)}, u32[]{:S(2)}) %collective-permute-start.34) | collective-permute-done | bytes 262176 | tf_op jit(solution)/shard_map/ppermute | solution.py:693
  185.0 6.5 %project_back.1 = (bf16[128,1024]{1,0:T(8,128)(2,1)}, bf16[128,1024]{1,0:T(8,128)(2,1)}, bf16[128,1024]{1,0:T(8,128)(2,1)}, bf16[128,1024]{1,0:T(8,128)(2,1)}, b...) custom-call(s32[3]{0:T(128)} %pad_add_fusion.scalars, ...), custom_call_target="tpu_custom_call" | custom-call | flops 1610612736 | bytes 7178240 | tf_op jit(solution)/shard_map/project_back/pallas_call | solution.py:60
  193.1 2.4 collective-permute-start.40
  208.4 8.1 %collective-permute-done.38.refs_1_ = bf16[128,1024]{1,0:T(8,128)(2,1)S(1)} collective-permute-done((bf16[128,1024]{1,0:T(8,128)(2,1)}, bf16[128,1024]{1,0:T(8,128)(2,1)S(1)}, u32[]{:S(2)}, u32[]{:S(2)}) %collective-permute-start.38) | collective-permute-done | bytes 262176 | tf_op jit(solution)/shard_map/ppermute | solution.py:693
  220.5 2.7 %collective-permute-start.43 = (bf16[160,1024]{1,0:T(8,128)(2,1)S(1)}, bf16[160,1024]{1,0:T(8,128)(2,1)S(1)}, u32[]{:S(2)}, u32[]{:S(2)}) collective-permute-start(bf16[160,1024]{1,0:T(8,128)(2,1)S(1)} %get-tuple-element.195), channel_id=1, source_target_pairs={{0,3},{1,2},{2,1},{3,0},{4,7},{5,6},{6,5},{7,4},{8,11},{9,10},{10,... | collective-permute-start | bytes 983048 | tf_op jit(solution)/shard_map/ppermute | solution.py:693
  226.6 4.0 %all-to-all-start = ((f32[32,8,128]{2,1,0:T(8,128)}), f32[32,8,128]{2,1,0:T(8,128)S(1)}, u32[]{:S(2)}, u32[]{:S(2)}) async-start(f32[32,8,128]{2,1,0:T(8,128)} %small.1), calls=%async_computation.2 | async-start | bytes 262144 | tf_op jit(solution)/shard_map/all_to_all | solution.py:1008
  230.6 12.7 %reduce-scatter.5.cloned.1.call-done.in_ref = bf16[128,768]{1,0:T(8,128)(2,1)} async-done(((bf16[1024,768]{1,0:T(8,128)(2,1)}), bf16[128,768]{1,0:T(8,128)(2,1)}) %reduce-scatter.5.cloned.1.call-update) | async-done | bytes 196624 | tf_op jit(solution)/shard_map/reduce_scatter | solution.py:958
  245.0 6.3 %collective-permute-done.42.refs_2_ = bf16[160,1024]{1,0:T(8,128)(2,1)S(1)} collective-permute-done((bf16[160,1024]{1,0:T(8,128)(2,1)S(1)}, bf16[160,1024]{1,0:T(8,128)(2,1)S(1)}, u32[]{:S(2)}, u32[]{:S(2)}) %collective-permute-start.42) | collective-permute-done | bytes 327712 | tf_op jit(solution)/shard_map/ppermute | solution.py:693
  (219 shorter events, 78.4 us)
Async XLA Ops:
  7.2 67.3 %all-gather.3.cloned.1.call-start = ((), (), s32[]{:S(2)}) async-start(), calls=%async_computation.5 | async-start | bytes 2162688 | tf_op jit(solution)/shard_map/all_gather | solution.py:741
  7.9 197.3 %reduce-scatter.3.cloned.1.call-start = ((), (), s32[]{:S(2)}) async-start(), calls=%async_computation.3 | async-start | bytes 7077888 | tf_op jit(solution)/shard_map/reduce_scatter | solution.py:958
  9.7 10.1 %collective-permute-start.2 = (bf16[136,768]{1,0:T(8,128)(2,1)}, bf16[136,768]{1,0:T(8,128)(2,1)S(1)}, u32[]{:S(2)}, u32[]{:S(2)}) collective-permute-start(bf16[136,768]{1,0:T(8,128)(2,1)} %pack.1.refs_0_.refs_2_), channel_id=1, source_target_pairs={{0,24},{4,28},{8,16},{12,20},{16,8},{20,12},{24,0},{28,4},{1,25},{... | collective-permute-start | bytes 626696 | tf_op jit(solution)/shard_map/ppermute | solution.py:687
  30.5 16.2 %collective-permute-start.8 = (bf16[512,512]{1,0:T(8,128)(2,1)}, bf16[512,512]{1,0:T(8,128)(2,1)S(1)}, u32[]{:S(2)}, u32[]{:S(2)}) collective-permute-start(bf16[512,512]{1,0:T(8,128)(2,1)} %get-tuple-element.119.refs_0_), channel_id=1, source_target_pairs={{0,8},{4,12},{8,0},{12,4},{1,9},{5,13},{9,1},{13,5},{2,10},{6,14},... | collective-permute-start | bytes 1572872 | tf_op jit(solution)/shard_map/ppermute | solution.py:690
  34.2 14.7 %collective-permute-start.11 = (bf16[256,1024]{1,0:T(8,128)(2,1)}, bf16[256,1024]{1,0:T(8,128)(2,1)S(1)}, u32[]{:S(2)}, u32[]{:S(2)}) collective-permute-start(bf16[256,1024]{1,0:T(8,128)(2,1)} %turn.1.refs_4_), channel_id=1, source_target_pairs={{0,4},{4,0},{8,12},{12,8},{1,5},{5,1},{9,13},{13,9},{2,6},{6,2},{1... | collective-permute-start | bytes 1572872 | tf_op jit(solution)/shard_map/ppermute | solution.py:690
  34.2 16.1 %collective-permute-start.10 = (bf16[256,1024]{1,0:T(8,128)(2,1)}, bf16[256,1024]{1,0:T(8,128)(2,1)S(1)}, u32[]{:S(2)}, u32[]{:S(2)}) collective-permute-start(bf16[256,1024]{1,0:T(8,128)(2,1)} %turn.1.refs_4_), channel_id=1, source_target_pairs={{0,16},{4,20},{8,24},{12,28},{16,0},{20,4},{24,8},{28,12},{1,17},{... | collective-permute-start | bytes 1572872 | tf_op jit(solution)/shard_map/ppermute | solution.py:687
  47.2 30.4 %collective-permute-start.18 = (bf16[256,1024]{1,0:T(8,128)(2,1)}, bf16[256,1024]{1,0:T(8,128)(2,1)S(1)}, u32[]{:S(2)}, u32[]{:S(2)}) collective-permute-start(bf16[256,1024]{1,0:T(8,128)(2,1)} %turn.1.refs_4_), channel_id=1, source_target_pairs={{0,24},{4,28},{8,16},{12,20},{16,8},{20,12},{24,0},{28,4},{1,25},{... | collective-permute-start | bytes 1572872 | tf_op jit(solution)/shard_map/ppermute | solution.py:687
  48.9 28.7 %collective-permute-start.17 = (bf16[256,1024]{1,0:T(8,128)(2,1)}, bf16[256,1024]{1,0:T(8,128)(2,1)S(1)}, u32[]{:S(2)}, u32[]{:S(2)}) collective-permute-start(bf16[256,1024]{1,0:T(8,128)(2,1)} %turn.1.refs_4_), channel_id=1, source_target_pairs={{0,8},{4,12},{8,0},{12,4},{16,24},{20,28},{24,16},{28,20},{1,9},{5... | collective-permute-start | bytes 1572872 | tf_op jit(solution)/shard_map/ppermute | solution.py:687
  77.6 16.4 %collective-permute-start.19 = (bf16[256,1024]{1,0:T(8,128)(2,1)S(1)}, bf16[256,1024]{1,0:T(8,128)(2,1)S(1)}, u32[]{:S(2)}, u32[]{:S(2)}) collective-permute-start(bf16[256,1024]{1,0:T(8,128)(2,1)S(1)} %collective-permute-done.17.refs_5_), channel_id=1, source_target_pairs={{0,4},{4,0},{8,12},{12,8},{1,5},{5,1},{9,13},{13,9},{2,6},{6,2},{1... | collective-permute-start | bytes 1572872 | tf_op jit(solution)/shard_map/ppermute | solution.py:690
  78.0 16.1 %collective-permute-start.20 = (bf16[256,1024]{1,0:T(8,128)(2,1)S(1)}, bf16[256,1024]{1,0:T(8,128)(2,1)S(1)}, u32[]{:S(2)}, u32[]{:S(2)}) collective-permute-start(bf16[256,1024]{1,0:T(8,128)(2,1)S(1)} %collective-permute-done.10.refs_6_), channel_id=1, source_target_pairs={{0,4},{4,0},{8,12},{12,8},{1,5},{5,1},{9,13},{13,9},{2,6},{6,2},{1... | collective-permute-start | bytes 1572872 | tf_op jit(solution)/shard_map/ppermute | solution.py:690
  78.2 15.8 %collective-permute-start.21 = (bf16[256,1024]{1,0:T(8,128)(2,1)S(1)}, bf16[256,1024]{1,0:T(8,128)(2,1)S(1)}, u32[]{:S(2)}, u32[]{:S(2)}) collective-permute-start(bf16[256,1024]{1,0:T(8,128)(2,1)S(1)} %collective-permute-done.18.refs_7_), channel_id=1, source_target_pairs={{0,4},{4,0},{8,12},{12,8},{1,5},{5,1},{9,13},{13,9},{2,6},{6,2},{1... | collective-permute-start | bytes 1572872 | tf_op jit(solution)/shard_map/ppermute | solution.py:690
  78.5 15.3 %collective-permute-start.15 = (bf16[128,1024]{1,0:T(8,128)(2,1)}, bf16[128,1024]{1,0:T(8,128)(2,1)S(1)}, u32[]{:S(2)}, u32[]{:S(2)}) collective-permute-start(bf16[128,1024]{1,0:T(8,128)(2,1)} %get-tuple-element.134.refs_0_), channel_id=1, source_target_pairs={{0,2},{1,3},{2,0},{3,1},{4,6},{5,7},{6,4},{7,5},{8,10},{9,11},{10,... | collective-permute-start | bytes 786440 | tf_op jit(solution)/shard_map/ppermute | solution.py:693
  80.4 13.6 %collective-permute-start.16 = (bf16[128,1024]{1,0:T(8,128)(2,1)}, bf16[128,1024]{1,0:T(8,128)(2,1)S(1)}, u32[]{:S(2)}, u32[]{:S(2)}) collective-permute-start(bf16[128,1024]{1,0:T(8,128)(2,1)} %get-tuple-element.134.refs_0_), channel_id=1, source_target_pairs={{0,1},{1,0},{2,3},{3,2},{4,5},{5,4},{6,7},{7,6},{8,9},{9,8},{10,11... | collective-permute-start | bytes 786440 | tf_op jit(solution)/shard_map/ppermute | solution.py:693
  98.6 17.3 %collective-permute-start.22 = (bf16[128,1024]{1,0:T(8,128)(2,1)S(1)}, bf16[128,1024]{1,0:T(8,128)(2,1)S(1)}, u32[]{:S(2)}, u32[]{:S(2)}) collective-permute-start(bf16[128,1024]{1,0:T(8,128)(2,1)S(1)} %get-tuple-element.142), channel_id=1, source_target_pairs={{0,2},{1,3},{2,0},{3,1},{4,6},{5,7},{6,4},{7,5},{8,10},{9,11},{10,... | collective-permute-start | bytes 786440 | tf_op jit(solution)/shard_map/ppermute | solution.py:693
  104.7 18.1 %collective-permute-start.24 = (bf16[128,1024]{1,0:T(8,128)(2,1)S(1)}, bf16[128,1024]{1,0:T(8,128)(2,1)S(1)}, u32[]{:S(2)}, u32[]{:S(2)}) collective-permute-start(bf16[128,1024]{1,0:T(8,128)(2,1)S(1)} %get-tuple-element.156), channel_id=1, source_target_pairs={{0,1},{1,0},{2,3},{3,2},{4,5},{5,4},{6,7},{7,6},{8,9},{9,8},{10,11... | collective-permute-start | bytes 786440 | tf_op jit(solution)/shard_map/ppermute | solution.py:693
  105.2 17.6 %collective-permute-start.25 = (bf16[128,1024]{1,0:T(8,128)(2,1)S(1)}, bf16[128,1024]{1,0:T(8,128)(2,1)S(1)}, u32[]{:S(2)}, u32[]{:S(2)}) collective-permute-start(bf16[128,1024]{1,0:T(8,128)(2,1)S(1)} %get-tuple-element.157), channel_id=1, source_target_pairs={{0,3},{1,2},{2,1},{3,0},{4,7},{5,6},{6,5},{7,4},{8,11},{9,10},{10,... | collective-permute-start | bytes 786440 | tf_op jit(solution)/shard_map/ppermute | solution.py:693
  129.2 114.1 %reduce-scatter.5.cloned.1.call-start = ((), (), s32[]{:S(2)}) async-start(), calls=%async_computation.4 | async-start | bytes 1769472 | tf_op jit(solution)/shard_map/reduce_scatter | solution.py:958
  135.1 13.7 %collective-permute-start.29 = (bf16[128,1024]{1,0:T(8,128)(2,1)S(1)}, bf16[128,1024]{1,0:T(8,128)(2,1)S(1)}, u32[]{:S(2)}, u32[]{:S(2)}) collective-permute-start(bf16[128,1024]{1,0:T(8,128)(2,1)S(1)} %copy-done.36), channel_id=1, source_target_pairs={{0,1},{1,0},{2,3},{3,2},{4,5},{5,4},{6,7},{7,6},{8,9},{9,8},{10,11... | collective-permute-start | bytes 786440 | tf_op jit(solution)/shard_map/ppermute | solution.py:693
  136.1 22.8 %collective-permute-start.30 = (bf16[128,1024]{1,0:T(8,128)(2,1)S(1)}, bf16[128,1024]{1,0:T(8,128)(2,1)S(1)}, u32[]{:S(2)}, u32[]{:S(2)}) collective-permute-start(bf16[128,1024]{1,0:T(8,128)(2,1)S(1)} %copy-done.32), channel_id=1, source_target_pairs={{0,2},{1,3},{2,0},{3,1},{4,6},{5,7},{6,4},{7,5},{8,10},{9,11},{10,... | collective-permute-start | bytes 786440 | tf_op jit(solution)/shard_map/ppermute | solution.py:693
  138.0 20.9 %collective-permute-start.31 = (bf16[128,1024]{1,0:T(8,128)(2,1)S(1)}, bf16[128,1024]{1,0:T(8,128)(2,1)S(1)}, u32[]{:S(2)}, u32[]{:S(2)}) collective-permute-start(bf16[128,1024]{1,0:T(8,128)(2,1)S(1)} %copy-done.34), channel_id=1, source_target_pairs={{0,3},{1,2},{2,1},{3,0},{4,7},{5,6},{6,5},{7,4},{8,11},{9,10},{10,... | collective-permute-start | bytes 786440 | tf_op jit(solution)/shard_map/ppermute | solution.py:693
  158.9 11.3 %collective-permute-start.36 = (bf16[512,512]{1,0:T(8,128)(2,1)}, bf16[512,512]{1,0:T(8,128)(2,1)S(1)}, u32[]{:S(2)}, u32[]{:S(2)}) collective-permute-start(bf16[512,512]{1,0:T(8,128)(2,1)} %get-tuple-element.176), channel_id=1, source_target_pairs={{0,4},{4,0},{8,12},{12,8},{1,5},{5,1},{9,13},{13,9},{2,6},{6,2},{1... | collective-permute-start | bytes 1572872 | tf_op jit(solution)/shard_map/ppermute | solution.py:690
  163.0 21.2 %collective-permute-start.37 = (bf16[512,512]{1,0:T(8,128)(2,1)S(1)}, bf16[512,512]{1,0:T(8,128)(2,1)S(1)}, u32[]{:S(2)}, u32[]{:S(2)}) collective-permute-start(bf16[512,512]{1,0:T(8,128)(2,1)S(1)} %get-tuple-element.177), channel_id=1, source_target_pairs={{0,8},{4,12},{8,0},{12,4},{1,9},{5,13},{9,1},{13,5},{2,10},{6,14},... | collective-permute-start | bytes 1572872 | tf_op jit(solution)/shard_map/ppermute | solution.py:690
  164.8 17.3 %collective-permute-start.34 = (bf16[128,1024]{1,0:T(8,128)(2,1)S(1)}, bf16[128,1024]{1,0:T(8,128)(2,1)S(1)}, u32[]{:S(2)}, u32[]{:S(2)}) collective-permute-start(bf16[128,1024]{1,0:T(8,128)(2,1)S(1)} %get-tuple-element.173.refs_0_), channel_id=1, source_target_pairs={{0,2},{1,3},{2,0},{3,1},{4,6},{5,7},{6,4},{7,5},{8,10},{9,11},{10,... | collective-permute-start | bytes 786440 | tf_op jit(solution)/shard_map/ppermute | solution.py:693
  170.2 11.9 %collective-permute-start.33 = (bf16[128,1024]{1,0:T(8,128)(2,1)S(1)}, bf16[128,1024]{1,0:T(8,128)(2,1)S(1)}, u32[]{:S(2)}, u32[]{:S(2)}) collective-permute-start(bf16[128,1024]{1,0:T(8,128)(2,1)S(1)} %get-tuple-element.173.refs_0_), channel_id=1, source_target_pairs={{0,1},{1,0},{2,3},{3,2},{4,5},{5,4},{6,7},{7,6},{8,9},{9,8},{10,11... | collective-permute-start | bytes 786440 | tf_op jit(solution)/shard_map/ppermute | solution.py:693
  191.6 12.1 %collective-permute-start.35 = (bf16[128,1024]{1,0:T(8,128)(2,1)S(1)}, bf16[128,1024]{1,0:T(8,128)(2,1)S(1)}, u32[]{:S(2)}, u32[]{:S(2)}) collective-permute-start(bf16[128,1024]{1,0:T(8,128)(2,1)S(1)} %collective-permute-done.34.refs_2_), channel_id=1, source_target_pairs={{0,1},{1,0},{2,3},{3,2},{4,5},{5,4},{6,7},{7,6},{8,9},{9,8},{10,11... | collective-permute-start | bytes 786440 | tf_op jit(solution)/shard_map/ppermute | solution.py:693
  193.1 15.2 %collective-permute-start.40 = (bf16[128,1024]{1,0:T(8,128)(2,1)}, bf16[128,1024]{1,0:T(8,128)(2,1)S(1)}, u32[]{:S(2)}, u32[]{:S(2)}) collective-permute-start(bf16[128,1024]{1,0:T(8,128)(2,1)} %get-tuple-element.184.refs_3_), channel_id=1, source_target_pairs={{0,3},{1,2},{2,1},{3,0},{4,7},{5,6},{6,5},{7,4},{8,11},{9,10},{10,... | collective-permute-start | bytes 786440 | tf_op jit(solution)/shard_map/ppermute | solution.py:693
  195.5 20.9 %collective-permute-start.38 = (bf16[128,1024]{1,0:T(8,128)(2,1)}, bf16[128,1024]{1,0:T(8,128)(2,1)S(1)}, u32[]{:S(2)}, u32[]{:S(2)}) collective-permute-start(bf16[128,1024]{1,0:T(8,128)(2,1)} %get-tuple-element.182.refs_1_), channel_id=1, source_target_pairs={{0,1},{1,0},{2,3},{3,2},{4,5},{5,4},{6,7},{7,6},{8,9},{9,8},{10,11... | collective-permute-start | bytes 786440 | tf_op jit(solution)/shard_map/ppermute | solution.py:693
  196.1 22.7 %collective-permute-start.39 = (bf16[128,1024]{1,0:T(8,128)(2,1)}, bf16[128,1024]{1,0:T(8,128)(2,1)}, u32[]{:S(2)}, u32[]{:S(2)}) collective-permute-start(bf16[128,1024]{1,0:T(8,128)(2,1)} %get-tuple-element.183.refs_2_), channel_id=1, source_target_pairs={{0,2},{1,3},{2,0},{3,1},{4,6},{5,7},{6,4},{7,5},{8,10},{9,11},{10,... | collective-permute-start | bytes 786440 | tf_op jit(solution)/shard_map/ppermute | solution.py:693
  220.5 24.5 %collective-permute-start.43 = (bf16[160,1024]{1,0:T(8,128)(2,1)S(1)}, bf16[160,1024]{1,0:T(8,128)(2,1)S(1)}, u32[]{:S(2)}, u32[]{:S(2)}) collective-permute-start(bf16[160,1024]{1,0:T(8,128)(2,1)S(1)} %get-tuple-element.195), channel_id=1, source_target_pairs={{0,3},{1,2},{2,1},{3,0},{4,7},{5,6},{6,5},{7,4},{8,11},{9,10},{10,... | collective-permute-start | bytes 983048 | tf_op jit(solution)/shard_map/ppermute | solution.py:693
  223.2 21.8 %collective-permute-start.41 = (bf16[160,1024]{1,0:T(8,128)(2,1)S(1)}, bf16[160,1024]{1,0:T(8,128)(2,1)S(1)}, u32[]{:S(2)}, u32[]{:S(2)}) collective-permute-start(bf16[160,1024]{1,0:T(8,128)(2,1)S(1)} %get-tuple-element.193), channel_id=1, source_target_pairs={{0,1},{1,0},{2,3},{3,2},{4,5},{5,4},{6,7},{7,6},{8,9},{9,8},{10,11... | collective-permute-start | bytes 983048 | tf_op jit(solution)/shard_map/ppermute | solution.py:693
  223.2 28.1 %collective-permute-start.42 = (bf16[160,1024]{1,0:T(8,128)(2,1)S(1)}, bf16[160,1024]{1,0:T(8,128)(2,1)S(1)}, u32[]{:S(2)}, u32[]{:S(2)}) collective-permute-start(bf16[160,1024]{1,0:T(8,128)(2,1)S(1)} %get-tuple-element.194), channel_id=1, source_target_pairs={{0,2},{1,3},{2,0},{3,1},{4,6},{5,7},{6,4},{7,5},{8,10},{9,11},{10,... | collective-permute-start | bytes 983048 | tf_op jit(solution)/shard_map/ppermute | solution.py:693
  226.6 26.6 %all-to-all-start = ((f32[32,8,128]{2,1,0:T(8,128)}), f32[32,8,128]{2,1,0:T(8,128)S(1)}, u32[]{:S(2)}, u32[]{:S(2)}) async-start(f32[32,8,128]{2,1,0:T(8,128)} %small.1), calls=%async_computation.2 | async-start | bytes 262144 | tf_op jit(solution)/shard_map/all_to_all | solution.py:1008
  (77 other events, 810.8 us)
Sparse Core Ops, SparseCore 0:
  10.9 63.4 all-gather.2
  129.3 71.6 reduce-scatter.2
  204.7 38.5 reduce-scatter.4
